TPU v7x, 256 devices: a whole 4x4x8 slice. The times are simulated.
256 devices in a mesh: sub: 32 (over x, z), col: 8 (over y, core).
Axes of the slice: x: 4, y: 4, z: 8, core: 2. Of those that a mesh axis runs over, the one named last changes fastest.
Arguments:
- leaf_basis: bfloat16 [32, 8, 2048, 512], P('sub', 'col'), as said below
- transfers: bfloat16 [32, 8, 4, 512, 512], P('sub', 'col'), as said below
- couplings: bfloat16 [32, 8, 6, 512, 512], P('sub', 'col'), may hold values from -0.25 to 0.25
- partners: int32 [32, 8, 6], P('sub', 'col'), may hold values from 0 to 7
Outputs:
- q_leaf: bfloat16 [32, 8, 2048, 512], P('sub', 'col')
- root_triangle: bfloat16 [32, 8, 512, 512], P('sub', 'col')
- coupled: bfloat16 [32, 8, 6, 512, 512], P('sub', 'col')
Inputs may be any that keep to these rules, and one draw needn't show every extreme that they name: partners[s,c,k] names the leaf cluster (s, partners[s,c,k]) as column cluster; entries may repeat. Every transfer matrix is a positive diagonal plus a dense part; transfers[s,c,l] is equal for all s with the same s >> l. `leaf_basis`: every leaf basis has full column rank.
All inputs are finite; a program needn't handle non-finite values.
Results may differ from a plain program's by a relative error of at most 0.0063.
Values may be sent and summed in bfloat16 or wider, within the bound.
No kernel may reach another device: no remote copies, remote signals or barrier semaphores. Data moves between devices by JAX's collectives and lax.ppermute only.
A program may use at most 128 MiB of HBM per device.

v0:
```python
import jax
import jax.numpy as jnp
from jax import lax
from jax.sharding import PartitionSpec as P

highest = lax.Precision.HIGHEST


def from_partner(block, axis, stride):
    count = lax.axis_size(axis)
    route = []
    for low in range(count):
        high = low | 1 << stride
        if high != low and high < count:
            route += [(low, high), (high, low)]
    return lax.ppermute(block, axis, route)


def blocked_cholesky(matrix):
    order = matrix.shape[0]
    width = 128
    columns = []
    trailing = matrix
    for start in range(0, order, width):
        head = jnp.linalg.cholesky(trailing[:width, :width])
        lower_part = trailing[width:, :width]
        if lower_part.shape[0] > 0:
            panel = lax.linalg.triangular_solve(
                head, lower_part, left_side=False, lower=True, transpose_a=True
            )
            trailing = trailing[width:, width:] - jnp.dot(panel, panel.T, precision=highest)
            column_block = jnp.concatenate(
                [jnp.zeros((start, width), jnp.float32), head, panel], axis=0
            )
        else:
            column_block = jnp.concatenate([jnp.zeros((start, width), jnp.float32), head], axis=0)
        columns.append(column_block)
    return jnp.concatenate(columns, axis=1)


def select_gathered(rounded, slot_partners):
    empty = jnp.zeros((slot_partners.shape[0],) + rounded.shape, jnp.bfloat16)
    chosen = empty
    pieces = lax.all_gather(rounded[None], "col", axis=0, tiled=True)
    offset = jnp.int32(0)
    for number in range(pieces.shape[0]):
        hit = (slot_partners == offset + number)[:, None, None]
        chosen = jnp.where(hit, pieces[number][None], chosen)
    return chosen


def project(rounded, blocks, slot_partners):
    left_product = jnp.einsum(
        "ab,kbd->kad", rounded, blocks, preferred_element_type=jnp.float32
    ).astype(jnp.bfloat16)
    chosen = select_gathered(rounded, slot_partners)
    return jnp.einsum(
        "kab,kdb->kad", left_product, chosen, preferred_element_type=jnp.float32
    ).astype(jnp.bfloat16)


def merge_levels(triangle, level_transfers):
    current = triangle
    contract = (((0,), (0,)), ((), ()))
    for level_index in range(level_transfers.shape[0]):
        moved = jnp.dot(
            current, level_transfers[level_index].astype(jnp.float32), precision=highest
        )
        own_gram = lax.dot_general(moved, moved, contract, precision=highest)
        partner_block = from_partner(moved, "sub", level_index)
        other_gram = lax.dot_general(partner_block, partner_block, contract, precision=highest)
        current = blocked_cholesky(own_gram + other_gram).T
    return current


def shards(leaf_basis, transfers, couplings, partners):
    own_basis = leaf_basis[0, 0]
    gram_leaf = lax.dot_general(
        own_basis, own_basis, (((0,), (0,)), ((), ())), preferred_element_type=jnp.float32
    )
    lower_leaf = blocked_cholesky(gram_leaf)
    q_transposed = lax.linalg.triangular_solve(
        lower_leaf, own_basis.T.astype(jnp.float32), left_side=True, lower=True
    )
    q_leaf = q_transposed.T.astype(jnp.bfloat16)
    triangle = lower_leaf.T
    rounded = triangle.astype(jnp.bfloat16)
    current = merge_levels(triangle, transfers[0, 0])
    coupled = project(rounded, couplings[0, 0], partners[0, 0])
    root_triangle = current.astype(jnp.bfloat16)
    return (q_leaf[None, None], root_triangle[None, None], coupled[None, None])


def solution(mesh):
    in_specs = (
        P("sub", "col", None, None),
        P("sub", "col", None, None, None),
        P("sub", "col", None, None, None),
        P("sub", "col", None),
    )
    out_specs = (
        P("sub", "col", None, None),
        P("sub", "col", None, None),
        P("sub", "col", None, None, None),
    )
    return jax.shard_map(shards, mesh=mesh, in_specs=in_specs, out_specs=out_specs, check_vma=False)
```

profile of v0, /device:TPU:12, one launch (start us, length us, event | category | flops | bytes accessed | tf_op | source)
XLA Modules:
  0.0 891.5 jit_solution(9750495935604740467)
XLA Ops:
  7.2 3.6 fusion.43
  15.1 11.7 %cholesky.314 = f32[128,128]{1,0:T(8,128)S(1)} custom-call(f32[128,128]{1,0:T(8,128)S(1)} %fusion.189), custom_call_target="Cholesky" | custom-call | tf_op jit(solution)/shard_map/jit(cholesky)/cholesky | solution.py:25
  28.8 9.8 %custom-call.27 = f32[1,128,128]{1,2,0:T(8,128)S(1)} custom-call(f32[1,128,128]{2,1,0:T(8,128)S(1)} %get-tuple-element.48), custom_call_target="InvertDiagBlocksLowerTriangular" | custom-call | tf_op jit(solution)/shard_map/triangular_solve/custom-call.0 | solution.py:28
  43.3 11.7 %cholesky.325 = f32[128,128]{1,0:T(8,128)S(1)} custom-call(f32[128,128]{1,0:T(8,128)S(1)} %fusion.187), custom_call_target="Cholesky" | custom-call | tf_op jit(solution)/shard_map/jit(cholesky)/cholesky | solution.py:25
  57.0 9.9 %custom-call.28 = f32[1,128,128]{1,2,0:T(8,128)S(1)} custom-call(f32[1,128,128]{2,1,0:T(8,128)S(1)} %get-tuple-element.46), custom_call_target="InvertDiagBlocksLowerTriangular" | custom-call | tf_op jit(solution)/shard_map/triangular_solve/custom-call.2 | solution.py:28
  73.3 12.5 %cholesky.336 = f32[128,128]{1,0:T(8,128)S(1)} custom-call(f32[128,128]{1,0:T(8,128)} %fusion.185), custom_call_target="Cholesky" | custom-call | tf_op jit(solution)/shard_map/jit(cholesky)/cholesky | solution.py:25
  87.9 11.3 %custom-call.29 = f32[1,128,128]{1,2,0:T(8,128)} custom-call(f32[1,128,128]{2,1,0:T(8,128)} %get-tuple-element.44), custom_call_target="InvertDiagBlocksLowerTriangular" | custom-call | tf_op jit(solution)/shard_map/triangular_solve/custom-call.3 | solution.py:28
  105.1 13.6 %cholesky.347 = f32[128,128]{1,0:T(8,128)} custom-call(f32[128,128]{1,0:T(8,128)} %fusion.183), custom_call_target="Cholesky" | custom-call | tf_op jit(solution)/shard_map/jit(cholesky)/cholesky | solution.py:25
  130.0 13.5 %while.1 = (s32[]{:T(128)}, f32[512,512]{1,0:T(8,128)}, s32[4,2]{0,1:T(2,128)S(1)}, f32[4,128,128]{2,1,0:T(8,128)}, s32[]{:T(128)}) while((s32[]{:T(128)}, f32[512,512]{1,0:T(8,128)}, s32[4,2]{0,1:T(2,128)S(1)}, f32[4,128,128]{2,1,0:T(8,128)}, s32[]{:T(128)}) %tuple.62), condition=%wide.while_cond, body=%wide.while_body.sunk | while | flops 2 | bytes 132205 | solution.py:82
  143.6 40.7 %custom-call.14 = f32[4,128,128]{1,2,0:T(8,128)} custom-call(f32[4,128,128]{2,1,0:T(8,128)} %get-tuple-element.14), custom_call_target="InvertDiagBlocksLowerTriangular" | custom-call | tf_op jit(solution)/shard_map/triangular_solve | solution.py:82
  190.4 3.6 convolution_add_fusion.3
  198.7 13.2 %cholesky.358 = f32[128,128]{1,0:T(8,128)} custom-call(f32[128,128]{1,0:T(8,128)} %fusion.182), custom_call_target="Cholesky" | custom-call | tf_op jit(solution)/shard_map/jit(cholesky)/cholesky | solution.py:25
  215.4 11.3 %custom-call.30 = f32[1,128,128]{1,2,0:T(8,128)} custom-call(f32[1,128,128]{2,1,0:T(8,128)} %get-tuple-element.42), custom_call_target="InvertDiagBlocksLowerTriangular" | custom-call | tf_op jit(solution)/shard_map/triangular_solve/custom-call.0 | solution.py:28
  235.1 13.3 %cholesky.369 = f32[128,128]{1,0:T(8,128)} custom-call(f32[128,128]{1,0:T(8,128)} %fusion.180), custom_call_target="Cholesky" | custom-call | tf_op jit(solution)/shard_map/jit(cholesky)/cholesky | solution.py:25
  252.1 11.3 %custom-call.31 = f32[1,128,128]{1,2,0:T(8,128)} custom-call(f32[1,128,128]{2,1,0:T(8,128)} %get-tuple-element.40), custom_call_target="InvertDiagBlocksLowerTriangular" | custom-call | tf_op jit(solution)/shard_map/triangular_solve/custom-call.2 | solution.py:28
  271.1 13.2 %cholesky.380 = f32[128,128]{1,0:T(8,128)} custom-call(f32[128,128]{1,0:T(8,128)} %fusion.178), custom_call_target="Cholesky" | custom-call | tf_op jit(solution)/shard_map/jit(cholesky)/cholesky | solution.py:25
  288.0 11.6 %custom-call.32 = f32[1,128,128]{1,2,0:T(8,128)} custom-call(f32[1,128,128]{2,1,0:T(8,128)} %get-tuple-element.38), custom_call_target="InvertDiagBlocksLowerTriangular" | custom-call | tf_op jit(solution)/shard_map/triangular_solve/custom-call.3 | solution.py:28
  306.2 13.2 %cholesky.391 = f32[128,128]{1,0:T(8,128)} custom-call(f32[128,128]{1,0:T(8,128)} %fusion.176), custom_call_target="Cholesky" | custom-call | tf_op jit(solution)/shard_map/jit(cholesky)/cholesky | solution.py:25
  339.0 34.4 %collective-permute-done.1 = f32[512,512]{1,0:T(8,128)S(1)} collective-permute-done((f32[512,512]{1,0:T(8,128)S(1)}, f32[512,512]{1,0:T(8,128)S(1)}, u32[]{:S(2)}, u32[]{:S(2)}) %collective-permute-start.1) | collective-permute-done | bytes 1048608 | tf_op jit(solution)/shard_map/ppermute | solution.py:16
  379.9 13.2 %cholesky.402 = f32[128,128]{1,0:T(8,128)} custom-call(f32[128,128]{1,0:T(8,128)} %fusion.175), custom_call_target="Cholesky" | custom-call | tf_op jit(solution)/shard_map/jit(cholesky)/cholesky | solution.py:25
  396.7 11.4 %custom-call.33 = f32[1,128,128]{1,2,0:T(8,128)} custom-call(f32[1,128,128]{2,1,0:T(8,128)} %get-tuple-element.36), custom_call_target="InvertDiagBlocksLowerTriangular" | custom-call | tf_op jit(solution)/shard_map/triangular_solve/custom-call.0 | solution.py:28
  416.4 13.2 %cholesky.413 = f32[128,128]{1,0:T(8,128)} custom-call(f32[128,128]{1,0:T(8,128)} %fusion.173), custom_call_target="Cholesky" | custom-call | tf_op jit(solution)/shard_map/jit(cholesky)/cholesky | solution.py:25
  433.1 11.3 %custom-call.34 = f32[1,128,128]{1,2,0:T(8,128)} custom-call(f32[1,128,128]{2,1,0:T(8,128)} %get-tuple-element.34), custom_call_target="InvertDiagBlocksLowerTriangular" | custom-call | tf_op jit(solution)/shard_map/triangular_solve/custom-call.2 | solution.py:28
  452.1 13.4 %cholesky.424 = f32[128,128]{1,0:T(8,128)} custom-call(f32[128,128]{1,0:T(8,128)} %fusion.171), custom_call_target="Cholesky" | custom-call | tf_op jit(solution)/shard_map/jit(cholesky)/cholesky | solution.py:25
  469.3 11.3 %custom-call.35 = f32[1,128,128]{1,2,0:T(8,128)} custom-call(f32[1,128,128]{2,1,0:T(8,128)} %get-tuple-element.32), custom_call_target="InvertDiagBlocksLowerTriangular" | custom-call | tf_op jit(solution)/shard_map/triangular_solve/custom-call.3 | solution.py:28
  487.1 13.2 %cholesky.435 = f32[128,128]{1,0:T(8,128)} custom-call(f32[128,128]{1,0:T(8,128)} %fusion.169), custom_call_target="Cholesky" | custom-call | tf_op jit(solution)/shard_map/jit(cholesky)/cholesky | solution.py:25
  506.1 6.4 collective-permute-start.2
  512.5 4.5 convolution_subtract_fusion
  519.8 7.3 fusion.31
  529.0 29.5 %collective-permute-done.2 = f32[512,512]{1,0:T(8,128)S(1)} collective-permute-done((f32[512,512]{1,0:T(8,128)S(1)}, f32[512,512]{1,0:T(8,128)S(1)}, u32[]{:S(2)}, u32[]{:S(2)}) %collective-permute-start.2) | collective-permute-done | bytes 1048608 | tf_op jit(solution)/shard_map/ppermute | solution.py:16
  565.3 13.2 %cholesky.446 = f32[128,128]{1,0:T(8,128)} custom-call(f32[128,128]{1,0:T(8,128)} %fusion.168), custom_call_target="Cholesky" | custom-call | tf_op jit(solution)/shard_map/jit(cholesky)/cholesky | solution.py:25
  582.1 11.3 %custom-call.36 = f32[1,128,128]{1,2,0:T(8,128)} custom-call(f32[1,128,128]{2,1,0:T(8,128)} %get-tuple-element.30), custom_call_target="InvertDiagBlocksLowerTriangular" | custom-call | tf_op jit(solution)/shard_map/triangular_solve/custom-call.0 | solution.py:28
  601.7 13.5 %cholesky.457 = f32[128,128]{1,0:T(8,128)} custom-call(f32[128,128]{1,0:T(8,128)} %fusion.166), custom_call_target="Cholesky" | custom-call | tf_op jit(solution)/shard_map/jit(cholesky)/cholesky | solution.py:25
  618.9 11.3 %custom-call.37 = f32[1,128,128]{1,2,0:T(8,128)} custom-call(f32[1,128,128]{2,1,0:T(8,128)} %get-tuple-element.28), custom_call_target="InvertDiagBlocksLowerTriangular" | custom-call | tf_op jit(solution)/shard_map/triangular_solve/custom-call.2 | solution.py:28
  637.9 13.2 %cholesky.468 = f32[128,128]{1,0:T(8,128)} custom-call(f32[128,128]{1,0:T(8,128)} %fusion.164), custom_call_target="Cholesky" | custom-call | tf_op jit(solution)/shard_map/jit(cholesky)/cholesky | solution.py:25
  654.8 11.3 %custom-call.38 = f32[1,128,128]{1,2,0:T(8,128)} custom-call(f32[1,128,128]{2,1,0:T(8,128)} %get-tuple-element.26), custom_call_target="InvertDiagBlocksLowerTriangular" | custom-call | tf_op jit(solution)/shard_map/triangular_solve/custom-call.3 | solution.py:28
  672.7 13.3 %cholesky.479 = f32[128,128]{1,0:T(8,128)} custom-call(f32[128,128]{1,0:T(8,128)} %fusion.162), custom_call_target="Cholesky" | custom-call | tf_op jit(solution)/shard_map/jit(cholesky)/cholesky | solution.py:25
  697.3 3.9 copy.70
  705.3 11.8 %collective-permute-done.3 = f32[512,512]{1,0:T(8,128)} collective-permute-done((f32[512,512]{1,0:T(8,128)}, f32[512,512]{1,0:T(8,128)}, u32[]{:S(2)}, u32[]{:S(2)}) %collective-permute-start.3) | collective-permute-done | bytes 1048608 | tf_op jit(solution)/shard_map/ppermute | solution.py:16
  725.2 13.2 %cholesky.490 = f32[128,128]{1,0:T(8,128)} custom-call(f32[128,128]{1,0:T(8,128)} %fusion.161), custom_call_target="Cholesky" | custom-call | tf_op jit(solution)/shard_map/jit(cholesky)/cholesky | solution.py:25
  742.2 11.3 %custom-call.39 = f32[1,128,128]{1,2,0:T(8,128)} custom-call(f32[1,128,128]{2,1,0:T(8,128)} %select_bitcast_fusion.2), custom_call_target="InvertDiagBlocksLowerTriangular" | custom-call | tf_op jit(solution)/shard_map/triangular_solve/custom-call.0 | solution.py:28
  761.8 13.6 %cholesky.501 = f32[128,128]{1,0:T(8,128)} custom-call(f32[128,128]{1,0:T(8,128)} %fusion.159), custom_call_target="Cholesky" | custom-call | tf_op jit(solution)/shard_map/jit(cholesky)/cholesky | solution.py:25
  779.0 11.3 %custom-call.40 = f32[1,128,128]{1,2,0:T(8,128)} custom-call(f32[1,128,128]{2,1,0:T(8,128)} %select_bitcast_fusion.1), custom_call_target="InvertDiagBlocksLowerTriangular" | custom-call | tf_op jit(solution)/shard_map/triangular_solve/custom-call.2 | solution.py:28
  797.9 13.2 %cholesky.512 = f32[128,128]{1,0:T(8,128)} custom-call(f32[128,128]{1,0:T(8,128)} %fusion.157), custom_call_target="Cholesky" | custom-call | tf_op jit(solution)/shard_map/jit(cholesky)/cholesky | solution.py:25
  814.8 11.3 %custom-call.41 = f32[1,128,128]{1,2,0:T(8,128)} custom-call(f32[1,128,128]{2,1,0:T(8,128)} %select_bitcast_fusion), custom_call_target="InvertDiagBlocksLowerTriangular" | custom-call | tf_op jit(solution)/shard_map/triangular_solve/custom-call.3 | solution.py:28
  832.8 13.2 %cholesky.523 = f32[128,128]{1,0:T(8,128)} custom-call(f32[128,128]{1,0:T(8,128)} %fusion.155), custom_call_target="Cholesky" | custom-call | tf_op jit(solution)/shard_map/jit(cholesky)/cholesky | solution.py:25
  855.8 4.2 fusion.209
  876.4 8.1 convert_bitcast_fusion
  (291 shorter events, 290.0 us)
Async XLA Ops:
  7.2 869.3 %copy-start = (bf16[1,1,6,512,512]{4,3,2,1,0:T(8,128)(2,1)S(1)}, bf16[1,1,6,512,512]{4,3,2,1,0:T(8,128)(2,1)}, u32[]{:S(2)}) copy-start(bf16[1,1,6,512,512]{4,3,2,1,0:T(8,128)(2,1)} %param.13) | copy-start | bytes 9437188
  7.2 848.6 %all-gather.3.cloned.1.call-start = ((), (), s32[]{:S(2)}) async-start(), calls=%async_computation | async-start | bytes 4718592 | tf_op jit(solution)/shard_map/all_gather | solution.py:44
  10.9 1.2 copy-start.31
  41.5 0.8 copy-start.11
  69.6 0.7 copy-start.26
  121.7 5.3 copy-start.38
  121.7 5.2 copy-start.25
  121.8 5.2 copy-start.35
  121.8 5.2 copy-start.36
  121.8 5.2 copy-start.37
  121.8 5.2 copy-start.39
  125.1 65.4 %collective-permute-start = (f32[512,512]{1,0:T(8,128)}, f32[512,512]{1,0:T(8,128)}, u32[]{:S(2)}, u32[]{:S(2)}) collective-permute-start(f32[512,512]{1,0:T(8,128)} %fusion.127), channel_id=1, source_target_pairs={{0,8},{8,0},{16,24},{24,16},{32,40},{40,32},{48,56},{56,48},{64,72... | collective-permute-start | bytes 3145736 | tf_op jit(solution)/shard_map/ppermute | solution.py:16
  184.3 3.6 copy-start.10
  194.1 1.0 copy-start.6
  228.2 0.7 copy-start.19
  230.6 0.8 copy-start.12
  264.7 0.6 copy-start.22
  266.7 0.7 copy-start.27
  300.8 0.6 copy-start.32
  320.9 7.3 copy-start.40
  324.9 48.5 %collective-permute-start.1 = (f32[512,512]{1,0:T(8,128)S(1)}, f32[512,512]{1,0:T(8,128)S(1)}, u32[]{:S(2)}, u32[]{:S(2)}) collective-permute-start(f32[512,512]{1,0:T(8,128)S(1)} %fusion.62), channel_id=1, source_target_pairs={{0,16},{16,0},{8,24},{24,8},{32,48},{48,32},{40,56},{56,40},{64,80... | collective-permute-start | bytes 3145736 | tf_op jit(solution)/shard_map/ppermute | solution.py:16
  330.7 1.1 copy-start.1
  375.2 1.0 copy-start.7
  409.6 0.7 copy-start.20
  412.0 0.8 copy-start.13
  445.7 0.7 copy-start.23
  447.7 0.7 copy-start.28
  481.7 0.6 copy-start.33
  501.8 10.8 %copy-start.2 = (f32[128,2048]{1,0:T(8,128)S(1)}, f32[128,2048]{1,0:T(8,128)}, u32[]{:S(2)}) copy-start(f32[128,2048]{1,0:T(8,128)} %copy-done.1) | copy-start | bytes 3145732
  501.8 10.8 %copy-start.3 = (f32[512,2048]{0,1:T(8,128)S(1)}, f32[512,2048]{0,1:T(8,128)}, u32[]{:S(2)}) copy-start(f32[512,2048]{0,1:T(8,128)} %bitcast_convert_fusion) | copy-start | bytes 12582916
  501.8 10.8 %copy-start.4 = (f32[128,2048]{1,0:T(8,128)S(1)}, f32[128,2048]{1,0:T(8,128)}, u32[]{:S(2)}) copy-start(f32[128,2048]{1,0:T(8,128)} %get-tuple-element.71) | copy-start | bytes 3145732
  506.1 52.4 %collective-permute-start.2 = (f32[512,512]{1,0:T(8,128)S(1)}, f32[512,512]{1,0:T(8,128)S(1)}, u32[]{:S(2)}, u32[]{:S(2)}) collective-permute-start(f32[512,512]{1,0:T(8,128)S(1)} %fusion.68), channel_id=1, source_target_pairs={{0,32},{32,0},{8,40},{40,8},{16,48},{48,16},{24,56},{56,24},{64,96... | collective-permute-start | bytes 3145736 | tf_op jit(solution)/shard_map/ppermute | solution.py:16
  560.6 1.0 copy-start.8
  594.8 0.7 copy-start.21
  597.2 0.8 copy-start.14
  631.5 0.6 copy-start.24
  633.5 0.7 copy-start.29
  667.3 0.6 copy-start.34
  687.5 6.3 copy-start.5
  689.1 6.6 copy-start.16
  689.1 6.6 copy-start.17
  689.1 6.6 copy-start.18
  692.6 24.5 %collective-permute-start.3 = (f32[512,512]{1,0:T(8,128)}, f32[512,512]{1,0:T(8,128)}, u32[]{:S(2)}, u32[]{:S(2)}) collective-permute-start(f32[512,512]{1,0:T(8,128)} %fusion.74), channel_id=1, source_target_pairs={{0,64},{64,0},{8,72},{72,8},{16,80},{80,16},{24,88},{88,24},{32,96... | collective-permute-start | bytes 3145736 | tf_op jit(solution)/shard_map/ppermute | solution.py:16
  697.3 3.9 copy-start.41
  720.6 1.0 copy-start.9
  757.2 0.8 copy-start.15
  793.5 0.7 copy-start.30
  864.1 12.4 %copy-start.42 = (pred[6]{0:T(512)(128)(4,1)S(1)}, pred[6]{0:T(512)(128)(4,1)}, u32[]{:S(2)}) copy-start(pred[6]{0:T(512)(128)(4,1)} %get-tuple-element.63) | copy-start | bytes 22
Sparse Core Ops, SparseCore 0:
  128.0 35.5 all-gather.2
where the time goes:
time: 907 us; the launch traced here: 892 us
  other arithmetic  576 us (64%)
  matrix products  115 us (13%)
  local copies, waits for them, and re-layouts  97.5 us (11%)
  waiting for transfers between devices  75.8 us (8%)
  between operations  15 us (2%)
  starting transfers between devices  12.9 us (1%)
    another operation x60, other arithmetic, blocked_cholesky(): head = jnp.linalg.cholesky(trailing[:width, :width])  290 us
    another operation x30, other arithmetic, blocked_cholesky(): lax.linalg.triangular_solve(head, lower_part, left_side=False, lower=True...  196 us
    ppermute x4, waiting for transfers between devices, from_partner(): return lax.ppermute(block, axis, route)  75.8 us
    another operation x3, other arithmetic, shards(): lax.linalg.triangular_solve(lower_leaf, own_basis.T.astype(jnp.float32),...  42.8 us
    div x20, other arithmetic, blocked_cholesky(): head = jnp.linalg.cholesky(trailing[:width, :width])  28.8 us
    slice x29, local copies, waits for them, and re-layouts, blocked_cholesky(): head = jnp.linalg.cholesky(trailing[:width, :width])  27.8 us
    unnamed x90, local copies, waits for them, and re-layouts  26.7 us
    another operation x7, matrix products, shards(): lax.linalg.triangular_solve(lower_leaf, own_basis.T.astype(jnp.float32),...  24.2 us
  transfers between devices with their start and end apart: 5, of which 3 were waited for; matrix products, arithmetic and copies ran while one was open for 70% of the time, Pallas kernels for 0%

commit v1 on v0

v1 whole, which is shorter than its diff:
```python
import jax
import jax.numpy as jnp
from jax import lax
from jax.experimental import pallas as pl
from jax.experimental.pallas import tpu as pltpu
from jax.sharding import PartitionSpec as P

f32, bf16 = jnp.float32, jnp.bfloat16
NN = ((1,), (0,))
TN = ((0,), (0,))
NT = ((1,), (1,))
SIDE = 128


def split(a):
    high = a.astype(bf16)
    return high, (a - high.astype(f32)).astype(bf16)


def dot(a, b, dims):
    return lax.dot_general(a, b, (dims, ((), ())), preferred_element_type=f32)


def dot3(a, b, dims):
    a_high, a_low = split(a)
    b_high, b_low = split(b)
    return dot(a_high, b_high, dims) + (dot(a_high, b_low, dims) + dot(a_low, b_high, dims))


def invert_lower(block):
    n = block.shape[0]
    parts = n // 8
    lane = lax.broadcasted_iota(jnp.int32, (8, n), 1)
    sub = lax.broadcasted_iota(jnp.int32, (8, n), 0)
    rows = [block[8 * t : 8 * t + 8, :] for t in range(parts)]
    result = []
    wide = lambda v: jnp.broadcast_to(v, (8, n))
    for t in range(parts):
        here = (lane >= 8 * t) & (lane < 8 * t + 8)
        current = rows[t]
        cols = [wide(current[:, 8 * t + k : 8 * t + k + 1]) for k in range(8)]
        work = jnp.where(here, (lane == sub + 8 * t).astype(f32), current)
        done = jnp.zeros((8, n), f32)
        scale = jnp.zeros((8, n), f32)
        for j in range(8):
            root = lax.rsqrt(wide(cols[j][j : j + 1, :]))
            inverse = root * root
            factor = jnp.where(sub == j, 0.0, cols[j]) * inverse
            pivot = wide(work[j : j + 1, :])
            done = jnp.where(sub == j, pivot * root, done)
            scale = jnp.where(sub == j, inverse, scale)
            work = work - factor * pivot
            for k in range(j + 1, 8):
                cols[k] = cols[k] - factor * wide(cols[k][j : j + 1, :])
        result.append(jnp.where(lane < 8 * t + 8, done, 0.0))
        if t + 1 < parts:
            scaled = work * scale
            lines = [wide(scaled[k : k + 1, :]) for k in range(8)]
            for s in range(t + 1, parts):
                total = jnp.where(here, 0.0, rows[s])
                for k in range(8):
                    total = total - wide(rows[s][:, 8 * t + k : 8 * t + k + 1]) * lines[k]
                rows[s] = total
    return jnp.concatenate(result, axis=0)


def factor_steps(x_ref, put_triangle, put_inverse):
    n = x_ref.shape[0]
    lane = lax.broadcasted_iota(jnp.int32, (SIDE, n), 1)
    sub = lax.broadcasted_iota(jnp.int32, (SIDE, n), 0)
    all_lane = lax.broadcasted_iota(jnp.int32, (n, n), 1)
    all_sub = lax.broadcasted_iota(jnp.int32, (n, n), 0)

    def step(k, carry):
        start = pl.multiple_of(k * SIDE, SIDE)
        at = pl.ds(start, SIDE)
        lower_inverse = invert_lower(x_ref[at, at])
        row = x_ref[at, :]
        here = (lane >= start) & (lane < start + SIDE)
        panel = dot3(lower_inverse, jnp.where(here, (lane == sub + start).astype(f32), row), NN)
        if put_inverse is not None:
            put_inverse(at, jnp.where(lane <= sub + start, panel, 0.0))
        put_triangle(at, jnp.where(lane >= sub + start, dot3(lower_inverse, row, NN), 0.0))
        change = dot3(jnp.where(lane >= start + SIDE, panel, 0.0), panel, TN)
        clear = (all_lane >= start) & (all_lane < start + SIDE) & (all_sub >= start + SIDE)
        x_ref[...] = jnp.where(clear, 0.0, x_ref[...]) - change
        return carry

    lax.fori_loop(0, n // SIDE, step, 0)


def leaf_kernel(gram_ref, rounded_ref, high_ref, low_ref, x_ref):
    x_ref[...] = gram_ref[...]

    def put_triangle(at, value):
        rounded_ref[at, :] = value.astype(bf16)

    def put_inverse(at, value):
        high, low = split(value)
        high_ref[at, :] = high
        low_ref[at, :] = low

    factor_steps(x_ref, put_triangle, put_inverse)


def root_kernel(gram_ref, root_ref, x_ref):
    x_ref[...] = gram_ref[...]

    def put_triangle(at, value):
        root_ref[at, :] = value.astype(bf16)

    factor_steps(x_ref, put_triangle, None)


def gram_kernel(basis_ref, transfer_ref, gram_ref, moved_ref):
    basis = basis_ref[...]
    gram = dot(basis, basis, TN)
    gram_ref[...] = gram
    path = transfer_ref[0].astype(f32)
    for level in range(1, transfer_ref.shape[0]):
        high, low = split(path)
        step = transfer_ref[level]
        path = dot(high, step, NN)
        if level > 1:
            path = path + dot(low, step, NN)
    moved_ref[...] = dot3(path, dot3(gram, path, NN), TN)


def basis_kernel(basis_ref, high_ref, low_ref, q_ref):
    basis = basis_ref[...]
    q_ref[...] = (dot(basis, high_ref[...], NT) + dot(basis, low_ref[...], NT)).astype(bf16)


def left_kernel(rounded_ref, block_ref, left_ref):
    left_ref[0] = dot(rounded_ref[...], block_ref[0], NN).astype(bf16)


def right_kernel(partner_ref, left_ref, chosen_ref, out_ref):
    del partner_ref
    out_ref[0] = dot(left_ref[0], chosen_ref[0], NT).astype(bf16)


def shards(leaf_basis, transfers, couplings, partners):
    basis, steps, blocks, picks = leaf_basis[0, 0], transfers[0, 0], couplings[0, 0], partners[0, 0]
    leaf, rank = basis.shape
    slots = blocks.shape[0]
    square = lambda dtype: jax.ShapeDtypeStruct((rank, rank), dtype)
    work = pltpu.VMEM((rank, rank), f32)
    gram, moved = pl.pallas_call(gram_kernel, out_shape=(square(f32), square(f32)), name="gram")(basis, steps)

    count = lax.axis_size("sub")
    group = 1 << steps.shape[0]
    groups = [list(range(low, low + group)) for low in range(0, count, group)]
    top = lax.psum(moved, "sub", axis_index_groups=groups)

    rounded, high, low = pl.pallas_call(
        leaf_kernel, out_shape=(square(bf16), square(bf16), square(bf16)), scratch_shapes=[work], name="leaf"
    )(gram)
    pieces = lax.all_gather(rounded, "col", axis=0)

    chunk = leaf // 4
    q_leaf = pl.pallas_call(
        basis_kernel,
        grid=(leaf // chunk,),
        in_specs=[
            pl.BlockSpec((chunk, rank), lambda i: (i, 0)),
            pl.BlockSpec((rank, rank), lambda i: (0, 0)),
            pl.BlockSpec((rank, rank), lambda i: (0, 0)),
        ],
        out_specs=pl.BlockSpec((chunk, rank), lambda i: (i, 0)),
        out_shape=jax.ShapeDtypeStruct((leaf, rank), bf16),
        name="basis",
    )(basis, high, low)
    left = pl.pallas_call(
        left_kernel,
        grid=(slots,),
        in_specs=[
            pl.BlockSpec((rank, rank), lambda k: (0, 0)),
            pl.BlockSpec((1, rank, rank), lambda k: (k, 0, 0)),
        ],
        out_specs=pl.BlockSpec((1, rank, rank), lambda k: (k, 0, 0)),
        out_shape=jax.ShapeDtypeStruct(blocks.shape, bf16),
        name="left",
    )(rounded, blocks)
    root = pl.pallas_call(root_kernel, out_shape=square(bf16), scratch_shapes=[work], name="root")(top)
    coupled = pl.pallas_call(
        right_kernel,
        grid_spec=pltpu.PrefetchScalarGridSpec(
            num_scalar_prefetch=1,
            grid=(slots,),
            in_specs=[
                pl.BlockSpec((1, rank, rank), lambda k, pick: (k, 0, 0)),
                pl.BlockSpec((1, rank, rank), lambda k, pick: (pick[k], 0, 0)),
            ],
            out_specs=pl.BlockSpec((1, rank, rank), lambda k, pick: (k, 0, 0)),
        ),
        out_shape=jax.ShapeDtypeStruct(blocks.shape, bf16),
        name="right",
    )(picks, left, pieces)
    return (q_leaf[None, None], root[None, None], coupled[None, None])


def solution(mesh):
    in_specs = (
        P("sub", "col", None, None),
        P("sub", "col", None, None, None),
        P("sub", "col", None, None, None),
        P("sub", "col", None),
    )
    out_specs = (
        P("sub", "col", None, None),
        P("sub", "col", None, None),
        P("sub", "col", None, None, None),
    )
    return jax.shard_map(shards, mesh=mesh, in_specs=in_specs, out_specs=out_specs, check_vma=False)
```

time: 907 us -> 196 us (0.22); the launches traced: 892 us -> 195 us
  other arithmetic: 576 us -> 0 us
  matrix products: 115 us -> 0 us
  local copies, waits for them, and re-layouts: 97.5 us -> 0 us
  Pallas kernels: 0 us -> 75 us
  waiting for transfers between devices: 75.8 us -> 105 us
  starting transfers between devices: 12.9 us -> 0.08 us
    another operation x95 -> x0, other arithmetic: 533 us -> none  [the longest x60 290 us: blocked_cholesky(): head = jnp.linalg.cholesky(trailing[:width, :width])]
    psum x0 -> x1, waiting for transfers between devices: none -> 105 us  [shards(): top = lax.psum(moved, 'sub', axis_index_groups=groups)]
    ppermute x4 -> x0, waiting for transfers between devices: 75.8 us -> none  [from_partner(): return lax.ppermute(block, axis, route)]
    pallas_call x0 -> x6, Pallas kernels: none -> 75 us  [the longest x1 24 us: shards(): pl.pallas_call(leaf_kernel, out_shape=(square(bf16), square(bf16), square...]
    dot_general x29 -> x0, matrix products: 68.9 us -> none  [the longest x15 23.9 us: blocked_cholesky(): jnp.dot(panel, panel.T, precision=highest)]
    slice x39 -> x0, local copies, waits for them, and re-layouts: 49.4 us -> none  [the longest x29 27.8 us: blocked_cholesky(): head = jnp.linalg.cholesky(trailing[:width, :width])]
    another operation x22 -> x0, matrix products: 45.7 us -> none  [the longest x7 24.2 us: shards(): lax.linalg.triangular_solve(lower_leaf, own_basis.T.astype(jnp.float32),...]
    div x20 -> x0, other arithmetic: 28.8 us -> none  [blocked_cholesky(): head = jnp.linalg.cholesky(trailing[:width, :width])]
  transfers between devices with their start and end apart: 5 -> 2, of which waited for: 3 -> 1; matrix products, arithmetic and copies ran while one was open for 70% -> 0% of each run, Pallas kernels for 0% -> 31%
where the time goes in v1:
time: 196 us; the launch traced here: 195 us
  waiting for transfers between devices  105 us (54%)
  Pallas kernels  75 us (38%)
  between operations  15.5 us (8%)
    psum x1, waiting for transfers between devices, shards(): top = lax.psum(moved, 'sub', axis_index_groups=groups)  105 us
    pallas_call x1, Pallas kernels, shards(): pl.pallas_call(leaf_kernel, out_shape=(square(bf16), square(bf16), square...  24 us
    pallas_call x1, Pallas kernels, shards(): pl.pallas_call(root_kernel, out_shape=square(bf16), scratch_shapes=[work]...  23.6 us
    pallas_call x1, Pallas kernels, shards(): pl.pallas_call(right_kernel, grid_spec=pltpu.PrefetchScalarGridSpec(num_s...  7.62 us
    pallas_call x1, Pallas kernels, shards(): pl.pallas_call(gram_kernel, out_shape=(square(f32), square(f32)), name='g...  7.6 us
    pallas_call x1, Pallas kernels, shards(): pl.pallas_call(left_kernel, grid=(slots,), in_specs=[pl.BlockSpec((rank,...  6.51 us
    pallas_call x1, Pallas kernels, shards(): pl.pallas_call(basis_kernel, grid=(leaf // chunk,), in_specs=[pl.BlockSpe...  5.69 us
  transfers between devices with their start and end apart: 2, of which 1 were waited for; matrix products, arithmetic and copies ran while one was open for 0% of the time, Pallas kernels for 31%

profile of v1, /device:TPU:12, one launch (start us, length us, event | category | flops | bytes accessed | tf_op | source)
XLA Modules:
  0.0 195.1 jit_solution(4940625307960843031)
XLA Ops:
  8.0 0.0 all-reduce.2.cloned.1.call-start
  8.0 7.6 %gram.1 = (f32[512,512]{1,0:T(8,128)}, f32[512,512]{1,0:T(8,128)}) custom-call(bf16[2048,512]{1,0:T(8,128)(2,1)} %bitcast.8, bf16[4,512,512]{2,1,0:T(8,128)(2,1)} %bitcast.13), custom_call_target="tpu_custom_call" | custom-call | tf_op jit(solution)/shard_map/gram/pallas_call | solution.py:149
  15.6 0.0 all-reduce.2.cloned.1.call-update
  15.7 0.0 all-gather.3.cloned.1.call-start
  15.7 24.0 %leaf.1 = (bf16[512,512]{1,0:T(8,128)(2,1)}, bf16[512,512]{1,0:T(8,128)(2,1)}, bf16[512,512]{1,0:T(8,128)(2,1)}) custom-call(f32[512,512]{1,0:T(8,128)} %get-tuple-element.8.gram_ref), custom_call_target="tpu_custom_call" | custom-call | tf_op jit(solution)/shard_map/leaf/pallas_call | solution.py:156
  39.8 0.0 all-gather.3.cloned.1.call-update
  39.8 6.5 %left.1.left_ref = bf16[6,512,512]{2,1,0:T(8,128)(2,1)} custom-call(bf16[512,512]{1,0:T(8,128)(2,1)} %get-tuple-element.12.rounded_ref, bf16[6,512,512]{2,1,0:T(8,128)(2,1)} %bitcast.11), custom_call_target="tpu_custom_call" | custom-call | tf_op jit(solution)/shard_map/left/pallas_call | solution.py:174
  46.3 5.7 %basis.1 = bf16[2048,512]{1,0:T(8,128)(2,1)} custom-call(bf16[2048,512]{1,0:T(8,128)(2,1)} %bitcast.9, bf16[512,512]{1,0:T(8,128)(2,1)} %get-tuple-element.9.high_ref, bf16[512,512]{1,0:T(8,128)(2,1)} %get-tuple-element.10.low_ref), custom_call_target="tpu_custom_call" | custom-call | tf_op jit(solution)/shard_map/basis/pallas_call | solution.py:162
  52.0 104.5 %all-reduce.2.cloned.1.call-done.gram_ref = f32[512,512]{1,0:T(8,128)} async-done(((f32[512,512]{1,0:T(8,128)}), f32[512,512]{1,0:T(8,128)}) %all-reduce.2.cloned.1.call-update) | async-done | bytes 1048592 | tf_op jit(solution)/shard_map/psum | solution.py:154
  156.5 23.6 %root.1 = bf16[512,512]{1,0:T(8,128)(2,1)} custom-call(f32[512,512]{1,0:T(8,128)} %all-reduce.2.cloned.1.call-done.gram_ref), custom_call_target="tpu_custom_call" | custom-call | tf_op jit(solution)/shard_map/root/pallas_call | solution.py:185
  180.1 0.0 all-gather.3.cloned.1.call-done
  180.1 7.6 %right.1 = bf16[6,512,512]{2,1,0:T(8,128)(2,1)} custom-call(s32[6]{0:T(128)} %bitcast.16, bf16[6,512,512]{2,1,0:T(8,128)(2,1)} %left.1.left_ref, bf16[8,512,512]{2,1,0:T(8,128)(2,1)} %bitcast.10), custom_call_target="tpu_custom_call" | custom-call | tf_op jit(solution)/shard_map/right/pallas_call | solution.py:186
Async XLA Ops:
  8.0 148.5 %all-reduce.2.cloned.1.call-start = ((), (), s32[]{:S(2)}) async-start(), calls=%async_computation | async-start | bytes 2097152 | tf_op jit(solution)/shard_map/psum | solution.py:154
  15.7 164.4 %all-gather.3.cloned.1.call-start = ((), (), s32[]{:S(2)}) async-start(), calls=%async_computation.1 | async-start | bytes 4718592 | tf_op jit(solution)/shard_map/all_gather | solution.py:159
Sparse Core Ops, SparseCore 0:
  15.8 140.6 all-reduce.1
Sparse Core Ops, SparseCore 1:
  39.9 36.3 all-gather.2

commit v2 on v1

--- a/solution.py
+++ b/solution.py
@@ -10,6 +10,7 @@
 TN = ((0,), (0,))
 NT = ((1,), (1,))
 SIDE = 128
+BASE = 16
 
 
 def split(a):
@@ -27,40 +28,60 @@
     return dot(a_high, b_high, dims) + (dot(a_high, b_low, dims) + dot(a_low, b_high, dims))
 
 
+def lane_of(rows, column):
+    return jnp.take_along_axis(rows, jnp.full(rows.shape, column, jnp.int32), axis=1)
+
+
 def invert_lower(block):
     n = block.shape[0]
     parts = n // 8
+    per = BASE // 8
     lane = lax.broadcasted_iota(jnp.int32, (8, n), 1)
     sub = lax.broadcasted_iota(jnp.int32, (8, n), 0)
     rows = [block[8 * t : 8 * t + 8, :] for t in range(parts)]
     result = []
     wide = lambda v: jnp.broadcast_to(v, (8, n))
-    for t in range(parts):
-        here = (lane >= 8 * t) & (lane < 8 * t + 8)
-        current = rows[t]
-        cols = [wide(current[:, 8 * t + k : 8 * t + k + 1]) for k in range(8)]
-        work = jnp.where(here, (lane == sub + 8 * t).astype(f32), current)
-        done = jnp.zeros((8, n), f32)
-        scale = jnp.zeros((8, n), f32)
-        for j in range(8):
-            root = lax.rsqrt(wide(cols[j][j : j + 1, :]))
-            inverse = root * root
-            factor = jnp.where(sub == j, 0.0, cols[j]) * inverse
-            pivot = wide(work[j : j + 1, :])
-            done = jnp.where(sub == j, pivot * root, done)
-            scale = jnp.where(sub == j, inverse, scale)
-            work = work - factor * pivot
-            for k in range(j + 1, 8):
-                cols[k] = cols[k] - factor * wide(cols[k][j : j + 1, :])
-        result.append(jnp.where(lane < 8 * t + 8, done, 0.0))
-        if t + 1 < parts:
-            scaled = work * scale
-            lines = [wide(scaled[k : k + 1, :]) for k in range(8)]
-            for s in range(t + 1, parts):
+    for first in range(0, parts, per):
+        group = range(first, first + per)
+        final = first + per >= parts
+        for t in group:
+            here = (lane >= 8 * t) & (lane < 8 * t + 8)
+            cols = [lane_of(rows[t], 8 * t + k) for k in range(8)]
+            work = jnp.where(here, (lane == sub + 8 * t).astype(f32), rows[t])
+            done = jnp.zeros((8, n), f32)
+            scale = jnp.zeros((8, n), f32)
+            for j in range(8):
+                root = lax.rsqrt(wide(cols[j][j : j + 1, :]))
+                inverse = root * root
+                factor = jnp.where(sub == j, 0.0, cols[j]) * inverse
+                pivot = wide(work[j : j + 1, :])
+                done = jnp.where(sub == j, pivot * root, done)
+                scale = jnp.where(sub == j, inverse, scale)
+                work = work - factor * pivot
+                for k in range(j + 1, 8):
+                    cols[k] = cols[k] - factor * wide(cols[k][j : j + 1, :])
+            result.append(jnp.where(lane < 8 * t + 8, done, 0.0))
+            if t + 1 == parts:
+                break
+            rows[t] = work * scale
+            lines = [wide(rows[t][k : k + 1, :]) for k in range(8)]
+            for s in group:
+                if s == t or (final and s < t):
+                    continue
                 total = jnp.where(here, 0.0, rows[s])
                 for k in range(8):
-                    total = total - wide(rows[s][:, 8 * t + k : 8 * t + k + 1]) * lines[k]
+                    total = total - lane_of(rows[s], 8 * t + k) * lines[k]
                 rows[s] = total
+        if not final:
+            low, high = 8 * first, 8 * (first + per)
+            solved = jnp.concatenate([rows[t] for t in group], axis=0)
+            rest = jnp.concatenate(rows[first + per :], axis=0)
+            lanes = lax.broadcasted_iota(jnp.int32, rest.shape, 1)
+            change = dot3(rest[:, low:high], solved, NN)
+            rest = jnp.where((lanes >= low) & (lanes < high), 0.0, rest) - change
+            for i in range(first + per, parts):
+                at = 8 * (i - first - per)
+                rows[i] = rest[at : at + 8, :]
     return jnp.concatenate(result, axis=0)
 
 
@@ -89,7 +110,12 @@
     lax.fori_loop(0, n // SIDE, step, 0)
 
 
-def leaf_kernel(gram_ref, rounded_ref, high_ref, low_ref, x_ref):
+def corners(n):
+    count = n // SIDE
+    return [(i, j) for i in range(count) for j in range(i, count)]
+
+
+def leaf_kernel(gram_ref, rounded_ref, packed_ref, high_ref, low_ref, x_ref):
     x_ref[...] = gram_ref[...]
 
     def put_triangle(at, value):
@@ -101,10 +127,17 @@
         low_ref[at, :] = low
 
     factor_steps(x_ref, put_triangle, put_inverse)
-
-
-def root_kernel(gram_ref, root_ref, x_ref):
-    x_ref[...] = gram_ref[...]
+    for number, (i, j) in enumerate(corners(gram_ref.shape[0])):
+        block = rounded_ref[i * SIDE : (i + 1) * SIDE, j * SIDE : (j + 1) * SIDE]
+        packed_ref[number * SIDE : (number + 1) * SIDE, :] = block
+
+
+def root_kernel(packed_ref, root_ref, x_ref):
+    for number, (i, j) in enumerate(corners(x_ref.shape[0])):
+        block = packed_ref[number * SIDE : (number + 1) * SIDE, :]
+        x_ref[i * SIDE : (i + 1) * SIDE, j * SIDE : (j + 1) * SIDE] = block
+        if i != j:
+            x_ref[j * SIDE : (j + 1) * SIDE, i * SIDE : (i + 1) * SIDE] = jnp.zeros((SIDE, SIDE), f32)
 
     def put_triangle(at, value):
         root_ref[at, :] = value.astype(bf16)
@@ -123,7 +156,17 @@
         path = dot(high, step, NN)
         if level > 1:
             path = path + dot(low, step, NN)
-    moved_ref[...] = dot3(path, dot3(gram, path, NN), TN)
+    n = gram.shape[0]
+    half = n // 2
+    carried = dot3(gram, path, NN)
+    upper = dot3(path[:, :half], carried, TN)
+    lower = dot3(path[:, half:], carried[:, half:], TN)
+    for number, (i, j) in enumerate(corners(n)):
+        if i * SIDE < half:
+            block = upper[i * SIDE : (i + 1) * SIDE, j * SIDE : (j + 1) * SIDE]
+        else:
+            block = lower[i * SIDE - half : (i + 1) * SIDE - half, j * SIDE - half : (j + 1) * SIDE - half]
+        moved_ref[number * SIDE : (number + 1) * SIDE, :] = block
 
 
 def basis_kernel(basis_ref, high_ref, low_ref, q_ref):
@@ -132,12 +175,23 @@
 
 
 def left_kernel(rounded_ref, block_ref, left_ref):
-    left_ref[0] = dot(rounded_ref[...], block_ref[0], NN).astype(bf16)
-
-
-def right_kernel(partner_ref, left_ref, chosen_ref, out_ref):
-    del partner_ref
-    out_ref[0] = dot(left_ref[0], chosen_ref[0], NT).astype(bf16)
+    half = rounded_ref.shape[0] // 2
+    left_ref[0, :half, :] = dot(rounded_ref[:half, :], block_ref[0], NN).astype(bf16)
+    left_ref[0, half:, :] = dot(rounded_ref[half:, half:], block_ref[0, half:, :], NN).astype(bf16)
+
+
+def right_kernel(place_ref, left_ref, mine_ref, other_ref, out_ref, full_ref):
+    n = full_ref.shape[0]
+    half = n // 2
+    swapped = place_ref[1, pl.program_id(0)] != 0
+    for number, (i, j) in enumerate(corners(n)):
+        at = slice(number * SIDE, (number + 1) * SIDE)
+        block = jnp.where(swapped, other_ref[0, at, :], mine_ref[0, at, :])
+        full_ref[i * SIDE : (i + 1) * SIDE, j * SIDE : (j + 1) * SIDE] = block
+        if i != j:
+            full_ref[j * SIDE : (j + 1) * SIDE, i * SIDE : (i + 1) * SIDE] = jnp.zeros((SIDE, SIDE), bf16)
+    out_ref[0, :, :half] = dot(left_ref[0], full_ref[:half, :], NT).astype(bf16)
+    out_ref[0, :, half:] = dot(left_ref[0, :, half:], full_ref[half:, half:], NT).astype(bf16)
 
 
 def shards(leaf_basis, transfers, couplings, partners):
@@ -145,19 +199,30 @@
     leaf, rank = basis.shape
     slots = blocks.shape[0]
     square = lambda dtype: jax.ShapeDtypeStruct((rank, rank), dtype)
+    tall = len(corners(rank)) * SIDE
+    packed_shape = lambda dtype: jax.ShapeDtypeStruct((tall, SIDE), dtype)
     work = pltpu.VMEM((rank, rank), f32)
-    gram, moved = pl.pallas_call(gram_kernel, out_shape=(square(f32), square(f32)), name="gram")(basis, steps)
+    gram, moved = pl.pallas_call(gram_kernel, out_shape=(square(f32), packed_shape(f32)), name="gram")(basis, steps)
 
     count = lax.axis_size("sub")
     group = 1 << steps.shape[0]
     groups = [list(range(low, low + group)) for low in range(0, count, group)]
-    top = lax.psum(moved, "sub", axis_index_groups=groups)
-
-    rounded, high, low = pl.pallas_call(
-        leaf_kernel, out_shape=(square(bf16), square(bf16), square(bf16)), scratch_shapes=[work], name="leaf"
+    shares = lax.all_to_all(moved.reshape(group, tall // group, SIDE), "sub", 0, 0, axis_index_groups=groups)
+    rounded, packed, high, low = pl.pallas_call(
+        leaf_kernel,
+        out_shape=(square(bf16), packed_shape(bf16), square(bf16), square(bf16)),
+        scratch_shapes=[work],
+        name="leaf",
     )(gram)
-    pieces = lax.all_gather(rounded, "col", axis=0)
-
+    shares, rounded, packed, high, low = lax.optimization_barrier((shares, rounded, packed, high, low))
+    share = jnp.sum(shares, axis=0)
+    top = lax.all_to_all(jnp.broadcast_to(share, shares.shape), "sub", 0, 0, axis_index_groups=groups)
+    top = top.reshape(tall, SIDE)
+
+    columns = lax.axis_size("col")
+    mine = [packed]
+    for shift in range(2, columns, 2):
+        mine.append(lax.ppermute(packed, "col", [(i, (i - shift) % columns) for i in range(columns)]))
     chunk = leaf // 4
     q_leaf = pl.pallas_call(
         basis_kernel,
@@ -182,21 +247,30 @@
         out_shape=jax.ShapeDtypeStruct(blocks.shape, bf16),
         name="left",
     )(rounded, blocks)
+    top, mine, left, q_leaf = lax.optimization_barrier((top, tuple(mine), left, q_leaf))
+    mine = jnp.stack(mine)
+    other = lax.ppermute(mine, "col", [(i, i ^ 1) for i in range(columns)])
+    top, mine = lax.optimization_barrier((top, mine))
+    here = lax.axis_index("col")
+    places = jnp.stack([((picks >> 1) - (here >> 1)) & (columns // 2 - 1), (picks ^ here) & 1])
     root = pl.pallas_call(root_kernel, out_shape=square(bf16), scratch_shapes=[work], name="root")(top)
+    root, other = lax.optimization_barrier((root, other))
     coupled = pl.pallas_call(
         right_kernel,
         grid_spec=pltpu.PrefetchScalarGridSpec(
             num_scalar_prefetch=1,
             grid=(slots,),
             in_specs=[
-                pl.BlockSpec((1, rank, rank), lambda k, pick: (k, 0, 0)),
-                pl.BlockSpec((1, rank, rank), lambda k, pick: (pick[k], 0, 0)),
+                pl.BlockSpec((1, rank, rank), lambda k, place: (k, 0, 0)),
+                pl.BlockSpec((1, tall, SIDE), lambda k, place: (place[0, k], 0, 0)),
+                pl.BlockSpec((1, tall, SIDE), lambda k, place: (place[0, k], 0, 0)),
             ],
-            out_specs=pl.BlockSpec((1, rank, rank), lambda k, pick: (k, 0, 0)),
+            out_specs=pl.BlockSpec((1, rank, rank), lambda k, place: (k, 0, 0)),
+            scratch_shapes=[pltpu.VMEM((rank, rank), bf16)],
         ),
         out_shape=jax.ShapeDtypeStruct(blocks.shape, bf16),
         name="right",
-    )(picks, left, pieces)
+    )(places, left, mine, other)
     return (q_leaf[None, None], root[None, None], coupled[None, None])
 
 

time: 196 us -> 99 us (0.51)
  the two profiles are of different devices: /device:TPU:12 before, /device:TPU:1 now
where the time goes in v2:
time: 99 us; the launch traced here: 98.2 us
  Pallas kernels  67 us (68%)
  starting transfers between devices  21.9 us (22%)
  waiting for transfers between devices  5.17 us (5%)
  local copies, waits for them, and re-layouts  2.65 us (3%)
    pallas_call x1, Pallas kernels, shards(): pl.pallas_call(leaf_kernel, out_shape=(square(bf16), packed_shape(bf16),...  20.4 us
    pallas_call x1, Pallas kernels, shards(): pl.pallas_call(root_kernel, out_shape=square(bf16), scratch_shapes=[work]...  19.5 us
    all_to_all x1, starting transfers between devices, shards(): lax.all_to_all(moved.reshape(group, tall // group, SIDE), 'sub', 0, 0, ax...  10 us
    pallas_call x1, Pallas kernels, shards(): pl.pallas_call(right_kernel, grid_spec=pltpu.PrefetchScalarGridSpec(num_s...  7.6 us
    all_to_all x1, starting transfers between devices, shards(): lax.all_to_all(jnp.broadcast_to(share, shares.shape), 'sub', 0, 0, axis_i...  7.56 us
    pallas_call x1, Pallas kernels, shards(): pl.pallas_call(gram_kernel, out_shape=(square(f32), packed_shape(f32)), n...  7.49 us
    pallas_call x1, Pallas kernels, shards(): pl.pallas_call(left_kernel, grid=(slots,), in_specs=[pl.BlockSpec((rank,...  6.27 us
    pallas_call x1, Pallas kernels, shards(): pl.pallas_call(basis_kernel, grid=(leaf // chunk,), in_specs=[pl.BlockSpe...  5.68 us
  transfers between devices with their start and end apart: 6, of which 1 were waited for; matrix products, arithmetic and copies ran while one was open for 1% of the time, Pallas kernels for 53%

profile of v2, /device:TPU:1, one launch (start us, length us, event | category | flops | bytes accessed | tf_op | source)
XLA Modules:
  0.0 98.2 jit_solution(3706488210595140064)
XLA Ops:
  0.6 7.5 %gram.1 = (f32[512,512]{1,0:T(8,128)}, f32[1280,128]{1,0:T(8,128)}) custom-call(bf16[2048,512]{1,0:T(8,128)(2,1)} %bitcast.16, bf16[4,512,512]{2,1,0:T(8,128)(2,1)} %bitcast.21), custom_call_target="tpu_custom_call" | custom-call | tf_op jit(solution)/shard_map/gram/pallas_call | solution.py:205
  8.1 10.0 %all-to-all-start = ((f32[16,80,128]{2,1,0:T(8,128)}), f32[16,80,128]{2,1,0:T(8,128)S(1)}, u32[]{:S(2)}, u32[]{:S(2)}) async-start(f32[16,80,128]{2,1,0:T(8,128)} %bitcast.23), calls=%async_computation | async-start | bytes 1310720 | tf_op jit(solution)/shard_map/all_to_all | solution.py:210
  18.2 20.4 %leaf.1 = (bf16[512,512]{1,0:T(8,128)(2,1)}, bf16[1280,128]{1,0:T(8,128)(2,1)}, bf16[512,512]{1,0:T(8,128)(2,1)}, bf16[512,512]{1,0:T(8,128)(2,1)}) custom-call(f32[512,512]{1,0:T(8,128)} %get-tuple-element.26.gram_ref), custom_call_target="tpu_custom_call" | custom-call | tf_op jit(solution)/shard_map/leaf/pallas_call | solution.py:211
  38.6 0.0 all-to-all-done
  38.6 0.0 copy-start.3
  38.7 0.9 broadcast_in_dim.12
  39.5 7.6 %all-to-all-start.1 = ((f32[16,80,128]{2,1,0:T(8,128)}), f32[16,80,128]{2,1,0:T(8,128)S(1)}, u32[]{:S(2)}, u32[]{:S(2)}) async-start(f32[16,80,128]{2,1,0:T(8,128)} %broadcast_in_dim.12), calls=%async_computation.1 | async-start | bytes 1310720 | tf_op jit(solution)/shard_map/all_to_all | solution.py:219
  47.1 0.0 copy-done.3
  47.1 2.8 %collective-permute-start = (bf16[1280,128]{1,0:T(8,128)(2,1)S(1)}, bf16[1280,128]{1,0:T(8,128)(2,1)S(1)}, u32[]{:S(2)}, u32[]{:S(2)}) collective-permute-start(bf16[1280,128]{1,0:T(8,128)(2,1)S(1)} %copy-done.3), channel_id=1, source_target_pairs={{0,6},{1,7},{2,0},{3,1},{4,2},{5,3},{6,4},{7,5},{8,14},{9,15},{10,... | collective-permute-start | bytes 983048 | tf_op jit(solution)/shard_map/ppermute | solution.py:225
  49.9 0.4 collective-permute-start.1
  50.3 0.7 collective-permute-start.2
  51.0 6.3 %left.1.left_ref = bf16[6,512,512]{2,1,0:T(8,128)(2,1)} custom-call(bf16[512,512]{1,0:T(8,128)(2,1)} %get-tuple-element.33.rounded_ref, bf16[6,512,512]{2,1,0:T(8,128)(2,1)} %bitcast.19), custom_call_target="tpu_custom_call" | custom-call | tf_op jit(solution)/shard_map/left/pallas_call | solution.py:239
  57.2 5.7 %basis.1 = bf16[2048,512]{1,0:T(8,128)(2,1)} custom-call(bf16[2048,512]{1,0:T(8,128)(2,1)} %bitcast.17, bf16[512,512]{1,0:T(8,128)(2,1)} %get-tuple-element.34.high_ref, bf16[512,512]{1,0:T(8,128)(2,1)} %get-tuple-element.35.low_ref), custom_call_target="tpu_custom_call" | custom-call | tf_op jit(solution)/shard_map/basis/pallas_call | solution.py:227
  62.9 0.0 collective-permute-done
  62.9 0.0 collective-permute-done.1
  62.9 5.2 %collective-permute-done.2 = bf16[1280,128]{1,0:T(8,128)(2,1)S(1)} collective-permute-done((bf16[1280,128]{1,0:T(8,128)(2,1)S(1)}, bf16[1280,128]{1,0:T(8,128)(2,1)S(1)}, u32[]{:S(2)}, u32[]{:S(2)}) %collective-permute-start.2) | collective-permute-done | bytes 327712 | tf_op jit(solution)/shard_map/ppermute | solution.py:225
  68.1 0.0 all-to-all-done.1
  68.1 0.0 copy-start.1
  68.1 0.0 copy-start.4
  68.1 0.2 pad_maximum_fusion.mine_ref
  68.3 0.7 copy-done.1
  68.9 0.0 copy-start
  68.9 0.5 collective-permute-start.3
  69.4 0.0 copy-done.4
  69.4 0.6 pad_add_fusion.place_ref
  70.0 19.5 %root.1 = bf16[512,512]{1,0:T(8,128)(2,1)} custom-call(f32[1280,128]{1,0:T(8,128)} %bitcast.20), custom_call_target="tpu_custom_call" | custom-call | tf_op jit(solution)/shard_map/root/pallas_call | solution.py:256
  89.5 0.0 collective-permute-done.3.other_ref
  89.5 0.0 copy-done
  89.5 0.0 copy-start.2
  89.5 1.1 %copy-done.2 = bf16[4,1280,128]{2,1,0:T(8,128)(2,1)} copy-done((bf16[4,1280,128]{2,1,0:T(8,128)(2,1)}, bf16[4,1280,128]{2,1,0:T(8,128)(2,1)S(1)}, u32[]{:S(2)}) %copy-start.2) | copy-done | bytes 1310744
  90.6 7.6 %right.1 = bf16[6,512,512]{2,1,0:T(8,128)(2,1)} custom-call(s32[2,6]{1,0:T(2,128)} %pad_add_fusion.place_ref, bf16[6,512,512]{2,1,0:T(8,128)(2,1)} %left.1.left_ref, bf16[4,1280,128]{2,1,0:T(8,128)(2,1)} %copy-done, bf16[4,1280,128]{2,1,0:T(8,128)(2,1)} %copy-done.2), custom_call_target="tpu_custom_call" | custom-call | tf_op jit(solution)/shard_map/right/pallas_call | solution.py:258
  (2 shorter events, 0.0 us)
Async XLA Ops:
  8.1 30.5 %all-to-all-start = ((f32[16,80,128]{2,1,0:T(8,128)}), f32[16,80,128]{2,1,0:T(8,128)S(1)}, u32[]{:S(2)}, u32[]{:S(2)}) async-start(f32[16,80,128]{2,1,0:T(8,128)} %bitcast.23), calls=%async_computation | async-start | bytes 1310720 | tf_op jit(solution)/shard_map/all_to_all | solution.py:210
  38.6 8.5 %copy-start.3 = (bf16[1280,128]{1,0:T(8,128)(2,1)S(1)}, bf16[1280,128]{1,0:T(8,128)(2,1)}, u32[]{:S(2)}) copy-start(bf16[1280,128]{1,0:T(8,128)(2,1)} %get-tuple-element.38) | copy-start | bytes 983044
  39.5 28.5 %all-to-all-start.1 = ((f32[16,80,128]{2,1,0:T(8,128)}), f32[16,80,128]{2,1,0:T(8,128)S(1)}, u32[]{:S(2)}, u32[]{:S(2)}) async-start(f32[16,80,128]{2,1,0:T(8,128)} %broadcast_in_dim.12), calls=%async_computation.1 | async-start | bytes 1310720 | tf_op jit(solution)/shard_map/all_to_all | solution.py:219
  47.1 15.8 %collective-permute-start = (bf16[1280,128]{1,0:T(8,128)(2,1)S(1)}, bf16[1280,128]{1,0:T(8,128)(2,1)S(1)}, u32[]{:S(2)}, u32[]{:S(2)}) collective-permute-start(bf16[1280,128]{1,0:T(8,128)(2,1)S(1)} %copy-done.3), channel_id=1, source_target_pairs={{0,6},{1,7},{2,0},{3,1},{4,2},{5,3},{6,4},{7,5},{8,14},{9,15},{10,... | collective-permute-start | bytes 983048 | tf_op jit(solution)/shard_map/ppermute | solution.py:225
  49.9 13.0 %collective-permute-start.1 = (bf16[1280,128]{1,0:T(8,128)(2,1)S(1)}, bf16[1280,128]{1,0:T(8,128)(2,1)S(1)}, u32[]{:S(2)}, u32[]{:S(2)}) collective-permute-start(bf16[1280,128]{1,0:T(8,128)(2,1)S(1)} %copy-done.3), channel_id=1, source_target_pairs={{0,4},{1,5},{2,6},{3,7},{4,0},{5,1},{6,2},{7,3},{8,12},{9,13},{10,... | collective-permute-start | bytes 983048 | tf_op jit(solution)/shard_map/ppermute | solution.py:225
  50.3 17.8 %collective-permute-start.2 = (bf16[1280,128]{1,0:T(8,128)(2,1)S(1)}, bf16[1280,128]{1,0:T(8,128)(2,1)S(1)}, u32[]{:S(2)}, u32[]{:S(2)}) collective-permute-start(bf16[1280,128]{1,0:T(8,128)(2,1)S(1)} %copy-done.3), channel_id=1, source_target_pairs={{0,2},{1,3},{2,4},{3,5},{4,6},{5,7},{6,0},{7,1},{8,10},{9,11},{10,... | collective-permute-start | bytes 983048 | tf_op jit(solution)/shard_map/ppermute | solution.py:225
  68.1 0.8 copy-start.1
  68.1 1.3 %copy-start.4 = (s32[1,1,6]{2,1,0:T(1,128)S(1)}, s32[1,1,6]{2,1,0:T(1,128)}, u32[]{:S(2)}) copy-start(s32[1,1,6]{2,1,0:T(1,128)} %param.7) | copy-start | bytes 76
  68.9 20.6 %copy-start = (bf16[4,1280,128]{2,1,0:T(8,128)(2,1)}, bf16[4,1280,128]{2,1,0:T(8,128)(2,1)S(1)}, u32[]{:S(2)}) copy-start(bf16[4,1280,128]{2,1,0:T(8,128)(2,1)S(1)} %pad_maximum_fusion.mine_ref) | copy-start | bytes 3932164
  68.9 20.6 %collective-permute-start.3 = (bf16[4,1280,128]{2,1,0:T(8,128)(2,1)S(1)}, bf16[4,1280,128]{2,1,0:T(8,128)(2,1)S(1)}, u32[]{:S(2)}, u32[]{:S(2)}) collective-permute-start(bf16[4,1280,128]{2,1,0:T(8,128)(2,1)S(1)} %pad_maximum_fusion.mine_ref), channel_id=1, source_target_pairs={{0,1},{1,0},{2,3},{3,2},{4,5},{5,4},{6,7},{7,6},{8,9},{9,8},{10,11... | collective-permute-start | bytes 3932168 | tf_op jit(solution)/shard_map/ppermute | solution.py:252
  89.5 1.1 %copy-start.2 = (bf16[4,1280,128]{2,1,0:T(8,128)(2,1)}, bf16[4,1280,128]{2,1,0:T(8,128)(2,1)S(1)}, u32[]{:S(2)}) copy-start(bf16[4,1280,128]{2,1,0:T(8,128)(2,1)S(1)} %collective-permute-done.3.other_ref) | copy-start | bytes 3932164

commit v3 on v0

v3 whole, which is shorter than its diff:
```python
import jax
import jax.numpy as jnp
from jax import lax
from jax.experimental import pallas as pl
from jax.experimental.pallas import tpu as pltpu
from jax.sharding import PartitionSpec as P


f32, bf16 = jnp.float32, jnp.bfloat16
NN = ((1,), (0,))
TN = ((0,), (0,))
NT = ((1,), (1,))
TT = ((0,), (1,))
SIDE = 128


def split(a):
    high = a.astype(bf16)
    return high, (a - high.astype(f32)).astype(bf16)


def dot(a, b, dims):
    return lax.dot_general(a, b, (dims, ((), ())), preferred_element_type=f32)


def product(a, b, dims):
    return dot(a[0], b[0], dims) + (dot(a[0], b[1], dims) + dot(a[1], b[0], dims))


def lane_of(rows, column):
    return jnp.take_along_axis(rows, jnp.full(rows.shape, column, jnp.int32), axis=1)


def invert_lower(block):
    n = block.shape[0]; parts = n // 8
    lane = lax.broadcasted_iota(jnp.int32, (8, n), 1)
    sub = lax.broadcasted_iota(jnp.int32, (8, n), 0)
    rows = [block[8*t:8*t+8, :] for t in range(parts)]
    result = []
    wide = lambda v: jnp.broadcast_to(v, (8, n))

    def pivots(t):
        here = (lane >= 8*t) & (lane < 8*t + 8)
        cols = [lane_of(rows[t], 8*t+k) for k in range(8)]
        work = jnp.where(here, (lane == sub + 8*t).astype(f32), rows[t])
        done = jnp.zeros((8, n), f32); scale = jnp.zeros((8, n), f32)
        for j in range(8):
            root = lax.rsqrt(wide(cols[j][j:j+1, :]))
            factor = jnp.where(sub == j, 0.0, cols[j]) * root
            for k in range(j+1, 8):
                cols[k] = cols[k] - factor * (wide(cols[k][j:j+1, :]) * root)
            pivot = wide(work[j:j+1, :]) * root
            done = jnp.where(sub == j, pivot, done)
            scale = jnp.where(sub == j, root * root, scale)
            work = work - factor * pivot
        result.append(jnp.where(lane < 8*t + 8, done, 0.0))
        rows[t] = work * scale
        return here, [wide(rows[t][k:k+1, :]) for k in range(8)]

    def apply(s, t, here, lines):
        terms = [lane_of(rows[s], 8*t+k) * lines[k] for k in range(8)]
        a = (terms[0] + terms[1]) + (terms[2] + terms[3])
        b = (terms[4] + terms[5]) + (terms[6] + terms[7])
        rows[s] = jnp.where(here, 0.0, rows[s]) - (a + b)

    for t in range(0, parts, 2):
        here, lines = pivots(t)
        apply(t+1, t, here, lines)
        more = t + 2 < parts
        if more: apply(t+2, t, here, lines)
        here, lines = pivots(t+1)
        if more:
            apply(t+2, t+1, here, lines)
            apply(t, t+1, here, lines)
        if t + 3 < parts:
            low, high = 8*t, 8*t+16
            solved = jnp.concatenate([rows[t], rows[t+1]], axis=0)
            rest = jnp.concatenate(rows[t+3:], axis=0)
            ln = lax.broadcasted_iota(jnp.int32, rest.shape, 1)
            change = product(split(rest[:, low:high]), split(solved), NN)
            rest = jnp.where((ln >= low) & (ln < high), 0.0, rest) - change
            for i in range(t+3, parts):
                rows[i] = rest[8*(i-t-3):8*(i-t-3)+8, :]
    return jnp.concatenate(result, axis=0)


def factor(x_ref, put_triangle, put_inverse, beside=None):
    n = x_ref.shape[0]; count = n // SIDE
    sub = lax.broadcasted_iota(jnp.int32, (SIDE, SIDE), 0)
    lane = lax.broadcasted_iota(jnp.int32, (SIDE, SIDE), 1)
    diagonal = x_ref[0:SIDE, 0:SIDE]
    for k in range(count):
        a, b = k*SIDE, (k+1)*SIDE
        if beside is not None:
            beside(k, count)
        inverse = invert_lower(diagonal)
        inv2 = split(inverse)
        put_triangle(k, k, jnp.where(lane >= sub, product(inv2, split(diagonal), NN), 0.0))
        right = []
        for j in range(k+1, count):
            piece = product(inv2, split(x_ref[a:b, j*SIDE:(j+1)*SIDE]), NN)
            put_triangle(k, j, piece)
            right.append(split(piece))
            if j == k+1:
                diagonal = x_ref[b:b+SIDE, b:b+SIDE] - product(right[0], right[0], TN)
        left = []
        if put_inverse is not None:
            for j in range(k):
                piece = product(inv2, split(x_ref[a:b, j*SIDE:(j+1)*SIDE]), NN)
                put_inverse(k, j, piece)
                left.append(split(piece))
            put_inverse(k, k, inverse)
            left.append(inv2)
        for i in range(k+1, count):
            side = right[i-k-1]
            at = slice(i*SIDE, (i+1)*SIDE)
            for j in range(max(i, k+2), count):
                to = slice(j*SIDE, (j+1)*SIDE)
                x_ref[at, to] = x_ref[at, to] - product(side, right[j-k-1], TN)
            for j in range(len(left)):
                to = slice(j*SIDE, (j+1)*SIDE)
                change = product(side, left[j], TN)
                x_ref[at, to] = -change if j == k else x_ref[at, to] - change


def corners(n):
    count = n // SIDE
    return [(i, j) for i in range(count) for j in range(i, count)]


def block_slice(i):
    return slice(i * SIDE, (i + 1) * SIDE)


def leaf_kernel(
    gram_ref, transfer_ref, rounded_ref, packed_ref, high_ref, low_ref, moved_ref, x_ref, path_ref, carried_ref
):
    n = x_ref.shape[0]
    half = n // 2
    levels = transfer_ref.shape[0]
    x_ref[...] = gram_ref[...]
    order = corners(n)
    empty = jnp.zeros((SIDE, SIDE), bf16)
    for i, j in order:
        if i != j:
            rounded_ref[block_slice(j), block_slice(i)] = empty
            high_ref[block_slice(i), block_slice(j)] = empty
            low_ref[block_slice(i), block_slice(j)] = empty

    def put_triangle(i, j, value):
        value = value.astype(bf16)
        rounded_ref[block_slice(i), block_slice(j)] = value
        packed_ref[block_slice(order.index((i, j))), :] = value

    def put_inverse(i, j, value):
        high_ref[block_slice(i), block_slice(j)], low_ref[block_slice(i), block_slice(j)] = split(value)

    def beside(k, count):
        if k == 0:
            path = split(dot(transfer_ref[levels - 1], transfer_ref[levels - 2], TT))
            for level in reversed(range(levels - 2)):
                step = transfer_ref[level]
                path = split(dot(path[0], step, NT) + dot(path[1], step, NT))
            path_ref[0], path_ref[1] = path
        elif k == 1:
            carried_ref[0], carried_ref[1] = split(product((path_ref[0], path_ref[1]), split(gram_ref[...]), NN))
        elif k == 2:
            top, low = slice(0, half), slice(half, n)
            upper = product((path_ref[0, top], path_ref[1, top]), (carried_ref[0], carried_ref[1]), NT)
            lower = product((path_ref[0, low], path_ref[1, low]), (carried_ref[0, low], carried_ref[1, low]), NT)
            most = jnp.maximum(
                jnp.max(upper[:, :half], axis=(0, 1), keepdims=True), jnp.max(lower, axis=(0, 1), keepdims=True)
            )
            exponent = jnp.broadcast_to(jnp.ceil(jnp.log2(most)) - 13.0, (8, SIDE))
            shrink = jnp.exp2(-exponent)
            sub = lax.broadcasted_iota(jnp.int32, (8, SIDE), 0)
            lane = lax.broadcasted_iota(jnp.int32, (8, SIDE), 1)
            for number, (i, j) in enumerate(order):
                for p in range(SIDE // 8):
                    row = i * SIDE + 8 * p
                    if row < half:
                        piece = upper[row : row + 8, block_slice(j)]
                    else:
                        piece = lower[row - half : row - half + 8, j * SIDE - half : (j + 1) * SIDE - half]
                    piece = piece * shrink
                    if number == 0:
                        piece = jnp.where((sub == 7) & (lane == 0), exponent, piece)
                    moved_ref[p, 8 * number : 8 * number + 8, :] = piece

    factor(x_ref, put_triangle, put_inverse, beside)


def root_kernel(pieces_ref, high_ref, low_ref, basis_ref, root_ref, q_ref, x_ref):
    n = x_ref.shape[0]
    empty = jnp.zeros((SIDE, SIDE), bf16)
    for number, (i, j) in enumerate(corners(n)):
        for p in range(SIDE // 8):
            at = slice(i * SIDE + 8 * p, i * SIDE + 8 * p + 8)
            x_ref[at, block_slice(j)] = pieces_ref[p, 8 * number : 8 * number + 8, :]
        if i != j:
            root_ref[block_slice(j), block_slice(i)] = empty
    first = x_ref[:SIDE, :SIDE]
    sub = lax.broadcasted_iota(jnp.int32, first.shape, 0)
    lane = lax.broadcasted_iota(jnp.int32, first.shape, 1)
    x_ref[:SIDE, :SIDE] = jnp.where((lane == 0) & (sub > 0), first.T, first)

    def put_triangle(i, j, value):
        root_ref[block_slice(i), block_slice(j)] = value.astype(bf16)

    half = n // 2

    def beside(k, count):
        rows = basis_ref.shape[0] // count
        at = slice(k * rows, (k + 1) * rows)
        for to, inner in ((slice(0, half), half), (slice(half, n), n)):
            part = basis_ref[at, :inner]
            q_ref[at, to] = (dot(part, high_ref[to, :inner], NT) + dot(part, low_ref[to, :inner], NT)).astype(bf16)

    factor(x_ref, put_triangle, None, beside)


def gram_kernel(basis_hbm, gram_ref, basis_ref, sems):
    parts, rows = basis_ref.shape[0], basis_ref.shape[1]
    loads = [
        pltpu.make_async_copy(basis_hbm.at[pl.ds(c * rows, rows), :], basis_ref.at[c], sems.at[c]) for c in range(parts)
    ]
    for load in loads:
        load.start()
    half = gram_ref.shape[0] // 2
    for c in range(parts):
        loads[c].wait()
        basis = basis_ref[c]
        upper = dot(basis[:, :half], basis, TN)
        lower = dot(basis[:, half:], basis[:, half:], TN)
        if c > 0:
            upper = gram_ref[:half, :] + upper
            lower = gram_ref[half:, half:] + lower
        gram_ref[:half, :] = upper
        gram_ref[half:, half:] = lower
    gram_ref[half:, :half] = gram_ref[:half, half:].T


def left_kernel(rounded_ref, block_hbm, left_hbm, block_ref, left_ref, sems):
    slots, n = block_ref.shape[0], block_ref.shape[1]
    half = n // 2
    loads = [pltpu.make_async_copy(block_hbm.at[k], block_ref.at[k], sems.at[0, k]) for k in range(slots)]
    stores = [pltpu.make_async_copy(left_ref.at[k], left_hbm.at[k], sems.at[1, k]) for k in range(slots)]
    for load in loads:
        load.start()
    for k in range(slots):
        loads[k].wait()
        left_ref[k, :half, :] = dot(rounded_ref[:half, :], block_ref[k], NN).astype(bf16)
        left_ref[k, half:, :] = dot(rounded_ref[half:, half:], block_ref[k, half:, :], NN).astype(bf16)
        stores[k].start()
    for store in stores:
        store.wait()


def right_kernel(pick_ref, left_hbm, mine_hbm, other_hbm, out_hbm, left_ref, chosen_ref, out_ref, sems):
    slots, n = left_ref.shape[0], left_ref.shape[1]
    half = n // 2
    chips = mine_hbm.shape[0]
    here = lax.axis_index("col")
    for k in range(slots):
        pick = pick_ref[k]
        place = ((pick >> 1) - (here >> 1)) & (chips - 1)
        swapped = ((pick ^ here) & 1) != 0
        pltpu.make_async_copy(left_hbm.at[k], left_ref.at[k], sems.at[0, k]).start()

        @pl.when(swapped)
        def _():
            pltpu.make_async_copy(other_hbm.at[place], chosen_ref.at[k], sems.at[1, k]).start()

        @pl.when(jnp.logical_not(swapped))
        def _():
            pltpu.make_async_copy(mine_hbm.at[place], chosen_ref.at[k], sems.at[1, k]).start()

    order = corners(n)
    empty = jnp.zeros((SIDE, SIDE), bf16)
    stores = []
    for k in range(slots):
        pltpu.make_async_copy(left_hbm.at[k], left_ref.at[k], sems.at[0, k]).wait()
        pltpu.make_async_copy(mine_hbm.at[0], chosen_ref.at[k], sems.at[1, k]).wait()

        def row(i, start):
            blocks = [
                chosen_ref[k, block_slice(order.index((i, j))), :] if j >= i else empty
                for j in range(start, n // SIDE)
            ]
            return jnp.concatenate(blocks, axis=1)

        count = n // SIDE
        above = jnp.concatenate([row(i, 0) for i in range(count // 2)], axis=0)
        below = jnp.concatenate([row(i, count // 2) for i in range(count // 2, count)], axis=0)
        out_ref[k, :, :half] = dot(left_ref[k], above, NT).astype(bf16)
        out_ref[k, :, half:] = dot(left_ref[k, :, half:], below, NT).astype(bf16)
        stores.append(pltpu.make_async_copy(out_ref.at[k], out_hbm.at[k], sems.at[2, k]))
        stores[k].start()
    for store in stores:
        store.wait()


def shards(leaf_basis, transfers, couplings, partners):
    basis, steps, blocks, picks = leaf_basis[0, 0], transfers[0, 0], couplings[0, 0], partners[0, 0]
    leaf, rank = basis.shape
    levels = steps.shape[0]
    slots = blocks.shape[0]
    square = lambda dtype: jax.ShapeDtypeStruct((rank, rank), dtype)
    tall = len(corners(rank)) * SIDE
    work = pltpu.VMEM((rank, rank), f32)
    far = pl.BlockSpec(memory_space=pl.ANY)
    near = pl.BlockSpec(memory_space=pltpu.VMEM)
    group = 1 << levels
    share_shape = (SIDE // 8, tall * 8 // SIDE, SIDE)
    parts = 4
    gram = pl.pallas_call(
        gram_kernel,
        out_shape=square(f32),
        in_specs=[far],
        out_specs=near,
        scratch_shapes=[pltpu.VMEM((parts, leaf // parts, rank), bf16), pltpu.SemaphoreType.DMA((parts,))],
        name="gram",
    )(basis)
    pair = pltpu.VMEM((2, rank, rank), bf16)
    rounded, packed, high, low, moved = pl.pallas_call(
        leaf_kernel,
        out_shape=(
            square(bf16),
            jax.ShapeDtypeStruct((tall, SIDE), bf16),
            square(bf16),
            square(bf16),
            jax.ShapeDtypeStruct(share_shape, f32),
        ),
        scratch_shapes=[work, pair, pair],
        name="leaf",
    )(gram, steps)

    count = lax.axis_size("sub")
    groups = [list(range(low_end, low_end + group)) for low_end in range(0, count, group)]
    shares = lax.all_to_all(moved.astype(jnp.float16), "sub", 0, 0, axis_index_groups=groups)
    columns = lax.axis_size("col")
    mine = [packed]
    for shift in range(2, columns, 2):
        mine.append(lax.ppermute(packed, "col", [(i, (i - shift) % columns) for i in range(columns)]))
    exponents = shares[:, 7, 0].astype(f32)
    common = jnp.max(exponents) + 4.0
    share = jnp.sum(shares.astype(f32) * jnp.exp2(exponents - common)[:, None, None], axis=0).astype(jnp.float16)
    share, rounded = lax.optimization_barrier((share, rounded))
    top = lax.all_to_all(jnp.broadcast_to(share, shares.shape), "sub", 0, 0, axis_index_groups=groups)
    left = pl.pallas_call(
        left_kernel,
        out_shape=jax.ShapeDtypeStruct(blocks.shape, bf16),
        in_specs=[near, far],
        out_specs=far,
        scratch_shapes=[
            pltpu.VMEM(blocks.shape, bf16),
            pltpu.VMEM(blocks.shape, bf16),
            pltpu.SemaphoreType.DMA((2, slots)),
        ],
        name="left",
    )(rounded, blocks)
    mine, left = lax.optimization_barrier((tuple(mine), left))
    mine = jnp.stack(mine)
    other = lax.ppermute(mine, "col", [(i, i ^ 1) for i in range(columns)])
    top, mine, left = lax.optimization_barrier((top, mine, left))
    top = top.astype(f32) * jnp.exp2(common)
    root, q_leaf = pl.pallas_call(
        root_kernel,
        out_shape=(square(bf16), jax.ShapeDtypeStruct(basis.shape, bf16)),
        scratch_shapes=[work],
        name="root",
    )(top, high, low, basis)
    left, other, root, q_leaf = lax.optimization_barrier((left, other, root, q_leaf))
    coupled = pl.pallas_call(
        right_kernel,
        out_shape=jax.ShapeDtypeStruct(blocks.shape, bf16),
        in_specs=[pl.BlockSpec(memory_space=pltpu.SMEM), far, far, far],
        out_specs=far,
        scratch_shapes=[
            pltpu.VMEM(blocks.shape, bf16),
            pltpu.VMEM((slots, tall, SIDE), bf16),
            pltpu.VMEM(blocks.shape, bf16),
            pltpu.SemaphoreType.DMA((3, slots)),
        ],
        compiler_params=pltpu.CompilerParams(vmem_limit_bytes=24 << 20),
        name="right",
    )(picks, left, mine, other)
    return (q_leaf[None, None], root[None, None], coupled[None, None])


def solution(mesh):
    in_specs = (
        P("sub", "col", None, None),
        P("sub", "col", None, None, None),
        P("sub", "col", None, None, None),
        P("sub", "col", None),
    )
    out_specs = (
        P("sub", "col", None, None),
        P("sub", "col", None, None),
        P("sub", "col", None, None, None),
    )
    return jax.shard_map(shards, mesh=mesh, in_specs=in_specs, out_specs=out_specs, check_vma=False)
```

time: 907 us -> 99.5 us (0.11); the launches traced: 892 us -> 98.3 us
  other arithmetic: 576 us -> 5 us
  matrix products: 115 us -> 0 us
  local copies, waits for them, and re-layouts: 97.5 us -> 0.78 us
  waiting for transfers between devices: 75.8 us -> 18.3 us
  Pallas kernels: 0 us -> 50.5 us
  between operations: 15 us -> 1.59 us
  starting transfers between devices: 12.9 us -> 22.1 us
    another operation x95 -> x1, other arithmetic: 533 us -> 1.24 us  [shards(): mine = jnp.stack(mine)]
    ppermute x4, waiting for transfers between devices: 75.8 us -> 0.12 us  [the longest x3 0.12 us: shards(): lax.ppermute(packed, 'col', [(i, (i - shift) % columns) for i in range(co...]
    dot_general x29 -> x0, matrix products: 68.9 us -> none  [the longest x15 23.9 us: blocked_cholesky(): jnp.dot(panel, panel.T, precision=highest)]
    pallas_call x0 -> x5, Pallas kernels: none -> 50.5 us  [the longest x1 19.2 us: shards(): pl.pallas_call(leaf_kernel, out_shape=(square(bf16), jax.ShapeDtypeStruct...]
    slice x39 -> x0, local copies, waits for them, and re-layouts: 49.4 us -> none  [the longest x29 27.8 us: blocked_cholesky(): head = jnp.linalg.cholesky(trailing[:width, :width])]
    another operation x22 -> x0, matrix products: 45.7 us -> none  [the longest x7 24.2 us: shards(): lax.linalg.triangular_solve(lower_leaf, own_basis.T.astype(jnp.float32),...]
    div x20 -> x0, other arithmetic: 28.8 us -> none  [blocked_cholesky(): head = jnp.linalg.cholesky(trailing[:width, :width])]
    unnamed x90 -> x6, local copies, waits for them, and re-layouts: 26.7 us -> 0.01 us
  transfers between devices with their start and end apart: 5 -> 6, of which waited for: 3 -> 3; matrix products, arithmetic and copies ran while one was open for 70% -> 3% of each run, Pallas kernels for 0% -> 23%
where the time goes in v3:
time: 99.5 us; the launch traced here: 98.3 us
  Pallas kernels  50.5 us (51%)
  starting transfers between devices  22.1 us (22%)
  waiting for transfers between devices  18.3 us (18%)
  other arithmetic  5 us (5%)
  between operations  1.59 us (2%)
    pallas_call x1, Pallas kernels, shards(): pl.pallas_call(leaf_kernel, out_shape=(square(bf16), jax.ShapeDtypeStruct...  19.2 us
    pallas_call x1, Pallas kernels, shards(): pl.pallas_call(root_kernel, out_shape=(square(bf16), jax.ShapeDtypeStruct...  17 us
    all_to_all x1, waiting for transfers between devices, shards(): lax.all_to_all(jnp.broadcast_to(share, shares.shape), 'sub', 0, 0, axis_i...  11.8 us
    all_to_all x1, starting transfers between devices, shards(): lax.all_to_all(moved.astype(jnp.float16), 'sub', 0, 0, axis_index_groups=...  9.21 us
    all_to_all x1, starting transfers between devices, shards(): lax.all_to_all(jnp.broadcast_to(share, shares.shape), 'sub', 0, 0, axis_i...  7.84 us
    all_to_all x1, waiting for transfers between devices, shards(): lax.all_to_all(moved.astype(jnp.float16), 'sub', 0, 0, axis_index_groups=...  6.4 us
    pallas_call x1, Pallas kernels, shards(): pl.pallas_call(right_kernel, out_shape=jax.ShapeDtypeStruct(blocks.shape,...  5.27 us
    pallas_call x1, Pallas kernels, shards(): pl.pallas_call(left_kernel, out_shape=jax.ShapeDtypeStruct(blocks.shape,...  5.22 us
  transfers between devices with their start and end apart: 6, of which 3 were waited for; matrix products, arithmetic and copies ran while one was open for 3% of the time, Pallas kernels for 23%

profile of v3, /device:TPU:12, one launch (start us, length us, event | category | flops | bytes accessed | tf_op | source)
XLA Modules:
  0.0 98.3 jit_solution(90664639304931847)
XLA Ops:
  0.6 3.8 %gram.1.gram_ref = f32[512,512]{1,0:T(8,128)} custom-call(bf16[2048,512]{1,0:T(8,128)(2,1)} %bitcast.12), custom_call_target="tpu_custom_call" | custom-call | tf_op jit(solution)/shard_map/gram/pallas_call | solution.py:316
  4.4 19.2 %leaf.1 = (bf16[512,512]{1,0:T(8,128)(2,1)}, bf16[1280,128]{1,0:T(8,128)(2,1)}, bf16[512,512]{1,0:T(8,128)(2,1)}, bf16[512,512]{1,0:T(8,128)(2,1)}, f32[16,80,128]{2,1,0:T(8,128)}) custom-call(f32[512,512]{1,0:T(8,128)} %gram.1.gram_ref, bf16[4,512,512]{2,1,0:T(8,128)(2,1)} %bitcast.16), custom_call_target="tpu_custom_call" | custom-call | tf_op jit(solution)/shard_map/leaf/pallas_call | solution.py:325
  23.6 0.0 copy-start.2
  23.6 1.9 %convert_element_type.17 = f16[16,80,128]{2,1,0:T(8,128)(2,1)} convert(f32[16,80,128]{2,1,0:T(8,128)} %get-tuple-element.24) | non-fusion elementwise | flops 163840 | bytes 983040 | tf_op jit(solution)/shard_map/convert_element_type | solution.py:340
  25.5 9.2 %all-to-all-start = ((f16[16,80,128]{2,1,0:T(8,128)(2,1)}), f16[16,80,128]{2,1,0:T(8,128)(2,1)S(1)}, u32[]{:S(2)}, u32[]{:S(2)}) async-start(f16[16,80,128]{2,1,0:T(8,128)(2,1)} %convert_element_type.17), calls=%async_computation | async-start | bytes 655360 | tf_op jit(solution)/shard_map/all_to_all | solution.py:340
  34.8 0.0 copy-done.2
  34.8 1.6 %collective-permute-start.2 = (bf16[1280,128]{1,0:T(8,128)(2,1)S(1)}, bf16[1280,128]{1,0:T(8,128)(2,1)S(1)}, u32[]{:S(2)}, u32[]{:S(2)}) collective-permute-start(bf16[1280,128]{1,0:T(8,128)(2,1)S(1)} %copy-done.2), channel_id=1, source_target_pairs={{0,2},{1,3},{2,4},{3,5},{4,6},{5,7},{6,0},{7,1},{8,10},{9,11},{10,... | collective-permute-start | bytes 983048 | tf_op jit(solution)/shard_map/ppermute | solution.py:344
  36.4 0.9 collective-permute-start.1
  37.4 2.4 %collective-permute-start = (bf16[1280,128]{1,0:T(8,128)(2,1)S(1)}, bf16[1280,128]{1,0:T(8,128)(2,1)S(1)}, u32[]{:S(2)}, u32[]{:S(2)}) collective-permute-start(bf16[1280,128]{1,0:T(8,128)(2,1)S(1)} %copy-done.2), channel_id=1, source_target_pairs={{0,6},{1,7},{2,0},{3,1},{4,2},{5,3},{6,4},{7,5},{8,14},{9,15},{10,... | collective-permute-start | bytes 983048 | tf_op jit(solution)/shard_map/ppermute | solution.py:344
  39.8 6.4 %all-to-all-done = f16[16,80,128]{2,1,0:T(8,128)(2,1)S(1)} async-done(((f16[16,80,128]{2,1,0:T(8,128)(2,1)}), f16[16,80,128]{2,1,0:T(8,128)(2,1)S(1)}, u32[]{:S(2)}, u32[]{:S(2)}) %all-to-all-start) | async-done | bytes 327712 | tf_op jit(solution)/shard_map/all_to_all | solution.py:340
  46.2 0.6 fusion
  47.4 0.2 exponential_reduce_fusion
  47.7 0.1 multiply_reduce_fusion
  47.8 5.2 %left.1.left_hbm = bf16[6,512,512]{2,1,0:T(8,128)(2,1)} custom-call(bf16[512,512]{1,0:T(8,128)(2,1)} %get-tuple-element.28.rounded_ref, bf16[6,512,512]{2,1,0:T(8,128)(2,1)} %bitcast.15), custom_call_target="tpu_custom_call" | custom-call | tf_op jit(solution)/shard_map/left/pallas_call | solution.py:350
  53.0 0.0 collective-permute-done.2
  53.0 0.0 collective-permute-done.1
  53.0 0.1 collective-permute-done
  53.2 1.2 %pad_maximum_fusion.mine_hbm = bf16[4,1280,128]{2,1,0:T(8,128)(2,1)} fusion(bf16[1,1280,128]{2,1,0:T(8,128)(2,1)S(1)} %bitcast.18, bf16[1,1280,128]{2,1,0:T(8,128)(2,1)S(1)} %bitcast.19, bf16[1,1280,128]{2,1,0:T(8,128)(2,1)S(1)} %bitcast.20, bf16[1,1280,128]{2,1,0:T(8,128)(2,1)S(1)} %bitcast.17), kind=kLoop, calls=%fused_computation | loop fusion | flops 1966080 | bytes 2621440 | tf_op jit(solution)/shard_map/stack | solution.py:363
  54.4 0.0 collective-permute-start.3
  54.4 0.8 broadcast_in_dim.13
  55.2 7.8 %all-to-all-start.1 = ((f16[16,80,128]{2,1,0:T(8,128)(2,1)}), f16[16,80,128]{2,1,0:T(8,128)(2,1)S(1)}, u32[]{:S(2)}, u32[]{:S(2)}) async-start(f16[16,80,128]{2,1,0:T(8,128)(2,1)} %broadcast_in_dim.13), calls=%async_computation.1 | async-start | bytes 655360 | tf_op jit(solution)/shard_map/all_to_all | solution.py:349
  63.1 11.8 %all-to-all-done.1 = f16[16,80,128]{2,1,0:T(8,128)(2,1)S(1)} async-done(((f16[16,80,128]{2,1,0:T(8,128)(2,1)}), f16[16,80,128]{2,1,0:T(8,128)(2,1)S(1)}, u32[]{:S(2)}, u32[]{:S(2)}) %all-to-all-start.1) | async-done | bytes 327712 | tf_op jit(solution)/shard_map/all_to_all | solution.py:349
  74.9 0.9 convert_multiply_fusion.pieces_ref
  75.8 0.0 copy-start
  75.8 0.0 copy-start.1
  75.8 17.0 %root.1 = (bf16[512,512]{1,0:T(8,128)(2,1)}, bf16[2048,512]{1,0:T(8,128)(2,1)}) custom-call(f32[16,80,128]{2,1,0:T(8,128)} %convert_multiply_fusion.pieces_ref, bf16[512,512]{1,0:T(8,128)(2,1)} %get-tuple-element.36.high_ref, bf16[512,512]{1,0:T(8,128)(2,1)} %get-tuple-element.37.low_ref, bf16[2048,512]{1,0:T(8,128)(2,1)} %bitcast.13), custom_call_target="tpu_custom_call" | custom-call | tf_op jit(solution)/shard_map/root/pallas_call | solution.py:367
  92.8 0.0 collective-permute-done.3.other_hbm
  92.8 0.0 copy-done
  92.8 0.0 copy-done.1
  92.8 5.3 %right.1 = bf16[6,512,512]{2,1,0:T(8,128)(2,1)} custom-call(s32[6]{0:T(128)S(1)} %bitcast.11, bf16[6,512,512]{2,1,0:T(8,128)(2,1)S(1)} %copy-done, bf16[4,1280,128]{2,1,0:T(8,128)(2,1)} %pad_maximum_fusion.mine_hbm, bf16[4,1280,128]{2,1,0:T(8,128)(2,1)} %collective-permute-done.3.other_hbm), custom_call_target="tpu_custom_call" | custom-call | tf_op jit(solution)/shard_map/right/pallas_call | solution.py:374
  (1 shorter events, 0.0 us)
Async XLA Ops:
  23.6 11.1 %copy-start.2 = (bf16[1280,128]{1,0:T(8,128)(2,1)S(1)}, bf16[1280,128]{1,0:T(8,128)(2,1)}, u32[]{:S(2)}) copy-start(bf16[1280,128]{1,0:T(8,128)(2,1)} %get-tuple-element.29) | copy-start | bytes 983044
  25.5 20.6 %all-to-all-start = ((f16[16,80,128]{2,1,0:T(8,128)(2,1)}), f16[16,80,128]{2,1,0:T(8,128)(2,1)S(1)}, u32[]{:S(2)}, u32[]{:S(2)}) async-start(f16[16,80,128]{2,1,0:T(8,128)(2,1)} %convert_element_type.17), calls=%async_computation | async-start | bytes 655360 | tf_op jit(solution)/shard_map/all_to_all | solution.py:340
  34.8 18.3 %collective-permute-start.2 = (bf16[1280,128]{1,0:T(8,128)(2,1)S(1)}, bf16[1280,128]{1,0:T(8,128)(2,1)S(1)}, u32[]{:S(2)}, u32[]{:S(2)}) collective-permute-start(bf16[1280,128]{1,0:T(8,128)(2,1)S(1)} %copy-done.2), channel_id=1, source_target_pairs={{0,2},{1,3},{2,4},{3,5},{4,6},{5,7},{6,0},{7,1},{8,10},{9,11},{10,... | collective-permute-start | bytes 983048 | tf_op jit(solution)/shard_map/ppermute | solution.py:344
  36.4 16.6 %collective-permute-start.1 = (bf16[1280,128]{1,0:T(8,128)(2,1)S(1)}, bf16[1280,128]{1,0:T(8,128)(2,1)S(1)}, u32[]{:S(2)}, u32[]{:S(2)}) collective-permute-start(bf16[1280,128]{1,0:T(8,128)(2,1)S(1)} %copy-done.2), channel_id=1, source_target_pairs={{0,4},{1,5},{2,6},{3,7},{4,0},{5,1},{6,2},{7,3},{8,12},{9,13},{10,... | collective-permute-start | bytes 983048 | tf_op jit(solution)/shard_map/ppermute | solution.py:344
  37.4 15.8 %collective-permute-start = (bf16[1280,128]{1,0:T(8,128)(2,1)S(1)}, bf16[1280,128]{1,0:T(8,128)(2,1)S(1)}, u32[]{:S(2)}, u32[]{:S(2)}) collective-permute-start(bf16[1280,128]{1,0:T(8,128)(2,1)S(1)} %copy-done.2), channel_id=1, source_target_pairs={{0,6},{1,7},{2,0},{3,1},{4,2},{5,3},{6,4},{7,5},{8,14},{9,15},{10,... | collective-permute-start | bytes 983048 | tf_op jit(solution)/shard_map/ppermute | solution.py:344
  54.4 38.4 %collective-permute-start.3 = (bf16[4,1280,128]{2,1,0:T(8,128)(2,1)}, bf16[4,1280,128]{2,1,0:T(8,128)(2,1)}, u32[]{:S(2)}, u32[]{:S(2)}) collective-permute-start(bf16[4,1280,128]{2,1,0:T(8,128)(2,1)} %pad_maximum_fusion.mine_hbm), channel_id=1, source_target_pairs={{0,1},{1,0},{2,3},{3,2},{4,5},{5,4},{6,7},{7,6},{8,9},{9,8},{10,11... | collective-permute-start | bytes 3932168 | tf_op jit(solution)/shard_map/ppermute | solution.py:364
  55.2 19.7 %all-to-all-start.1 = ((f16[16,80,128]{2,1,0:T(8,128)(2,1)}), f16[16,80,128]{2,1,0:T(8,128)(2,1)S(1)}, u32[]{:S(2)}, u32[]{:S(2)}) async-start(f16[16,80,128]{2,1,0:T(8,128)(2,1)} %broadcast_in_dim.13), calls=%async_computation.1 | async-start | bytes 655360 | tf_op jit(solution)/shard_map/all_to_all | solution.py:349
  75.8 17.0 %copy-start = (bf16[6,512,512]{2,1,0:T(8,128)(2,1)S(1)}, bf16[6,512,512]{2,1,0:T(8,128)(2,1)}, u32[]{:S(2)}) copy-start(bf16[6,512,512]{2,1,0:T(8,128)(2,1)} %left.1.left_hbm) | copy-start | bytes 9437188
  75.8 17.0 %copy-start.1 = (s32[1,1,6]{2,1,0:T(1,128)S(1)}, s32[1,1,6]{2,1,0:T(1,128)}, u32[]{:S(2)}) copy-start(s32[1,1,6]{2,1,0:T(1,128)} %param.7) | copy-start | bytes 76

commit v4 on v3

--- a/solution.py
+++ b/solution.py
@@ -84,12 +84,13 @@
     return jnp.concatenate(result, axis=0)
 
 
-def factor(x_ref, put_triangle, put_inverse, beside=None):
+def factor(x_ref, put_triangle, put_inverse, beside=None, first=0, last=None):
     n = x_ref.shape[0]; count = n // SIDE
     sub = lax.broadcasted_iota(jnp.int32, (SIDE, SIDE), 0)
     lane = lax.broadcasted_iota(jnp.int32, (SIDE, SIDE), 1)
-    diagonal = x_ref[0:SIDE, 0:SIDE]
-    for k in range(count):
+    last = count if last is None else last
+    diagonal = x_ref[first*SIDE:(first+1)*SIDE, first*SIDE:(first+1)*SIDE]
+    for k in range(first, last):
         a, b = k*SIDE, (k+1)*SIDE
         if beside is not None:
             beside(k, count)
@@ -103,6 +104,8 @@
             right.append(split(piece))
             if j == k+1:
                 diagonal = x_ref[b:b+SIDE, b:b+SIDE] - product(right[0], right[0], TN)
+                if j == last:
+                    x_ref[b:b+SIDE, b:b+SIDE] = diagonal
         left = []
         if put_inverse is not None:
             for j in range(k):
@@ -132,8 +135,8 @@
     return slice(i * SIDE, (i + 1) * SIDE)
 
 
-def leaf_kernel(
-    gram_ref, transfer_ref, rounded_ref, packed_ref, high_ref, low_ref, moved_ref, x_ref, path_ref, carried_ref
+def first_kernel(
+    gram_ref, transfer_ref, rounded_ref, packed_ref, high_ref, low_ref, moved_ref, state_ref, x_ref, path_ref, carried_ref
 ):
     n = x_ref.shape[0]
     half = n // 2
@@ -141,11 +144,9 @@
     x_ref[...] = gram_ref[...]
     order = corners(n)
     empty = jnp.zeros((SIDE, SIDE), bf16)
-    for i, j in order:
-        if i != j:
-            rounded_ref[block_slice(j), block_slice(i)] = empty
-            high_ref[block_slice(i), block_slice(j)] = empty
-            low_ref[block_slice(i), block_slice(j)] = empty
+    rounded_ref[block_slice(1), block_slice(0)] = empty
+    high_ref[block_slice(0), block_slice(1)] = empty
+    low_ref[block_slice(0), block_slice(1)] = empty
 
     def put_triangle(i, j, value):
         value = value.astype(bf16)
@@ -162,9 +163,8 @@
                 step = transfer_ref[level]
                 path = split(dot(path[0], step, NT) + dot(path[1], step, NT))
             path_ref[0], path_ref[1] = path
+            carried_ref[0], carried_ref[1] = split(product((path_ref[0], path_ref[1]), split(gram_ref[...]), NN))
         elif k == 1:
-            carried_ref[0], carried_ref[1] = split(product((path_ref[0], path_ref[1]), split(gram_ref[...]), NN))
-        elif k == 2:
             top, low = slice(0, half), slice(half, n)
             upper = product((path_ref[0, top], path_ref[1, top]), (carried_ref[0], carried_ref[1]), NT)
             lower = product((path_ref[0, low], path_ref[1, low]), (carried_ref[0, low], carried_ref[1, low]), NT)
@@ -187,10 +187,35 @@
                         piece = jnp.where((sub == 7) & (lane == 0), exponent, piece)
                     moved_ref[p, 8 * number : 8 * number + 8, :] = piece
 
-    factor(x_ref, put_triangle, put_inverse, beside)
-
-
-def root_kernel(pieces_ref, high_ref, low_ref, basis_ref, root_ref, q_ref, x_ref):
+    factor(x_ref, put_triangle, put_inverse, beside, last=n // SIDE // 2)
+    state_ref[...] = x_ref[half:, :]
+
+
+def second_kernel(state_ref, started_ref, rounded_ref, packed_ref, high_ref, low_ref, x_ref):
+    n = x_ref.shape[0]
+    half = n // 2
+    middle = half // SIDE
+    order = corners(n)
+    x_ref[half:, :] = state_ref[...]
+    packed_ref[: started_ref.shape[0], :] = started_ref[...]
+    empty = jnp.zeros((SIDE, SIDE), bf16)
+    rounded_ref[block_slice(1), block_slice(0)] = empty
+    high_ref[block_slice(0), block_slice(middle + 1)] = empty
+    low_ref[block_slice(0), block_slice(middle + 1)] = empty
+
+    def put_triangle(i, j, value):
+        value = value.astype(bf16)
+        rounded_ref[block_slice(i - middle), block_slice(j - middle)] = value
+        packed_ref[block_slice(order.index((i, j))), :] = value
+
+    def put_inverse(i, j, value):
+        at = block_slice(i - middle), block_slice(j)
+        high_ref[at], low_ref[at] = split(value)
+
+    factor(x_ref, put_triangle, put_inverse, first=middle)
+
+
+def root_kernel(pieces_ref, high_ref, low_ref, next_high_ref, next_low_ref, basis_ref, root_ref, q_ref, x_ref):
     n = x_ref.shape[0]
     empty = jnp.zeros((SIDE, SIDE), bf16)
     for number, (i, j) in enumerate(corners(n)):
@@ -212,9 +237,10 @@
     def beside(k, count):
         rows = basis_ref.shape[0] // count
         at = slice(k * rows, (k + 1) * rows)
-        for to, inner in ((slice(0, half), half), (slice(half, n), n)):
-            part = basis_ref[at, :inner]
-            q_ref[at, to] = (dot(part, high_ref[to, :inner], NT) + dot(part, low_ref[to, :inner], NT)).astype(bf16)
+        part = basis_ref[at, :half]
+        q_ref[at, :half] = (dot(part, high_ref[...], NT) + dot(part, low_ref[...], NT)).astype(bf16)
+        part = basis_ref[at, :]
+        q_ref[at, half:] = (dot(part, next_high_ref[...], NT) + dot(part, next_low_ref[...], NT)).astype(bf16)
 
     factor(x_ref, put_triangle, None, beside)
 
@@ -240,7 +266,7 @@
     gram_ref[half:, :half] = gram_ref[:half, half:].T
 
 
-def left_kernel(rounded_ref, block_hbm, left_hbm, block_ref, left_ref, sems):
+def left_kernel(rounded_ref, next_ref, block_hbm, left_hbm, block_ref, left_ref, sems):
     slots, n = block_ref.shape[0], block_ref.shape[1]
     half = n // 2
     loads = [pltpu.make_async_copy(block_hbm.at[k], block_ref.at[k], sems.at[0, k]) for k in range(slots)]
@@ -249,8 +275,8 @@
         load.start()
     for k in range(slots):
         loads[k].wait()
-        left_ref[k, :half, :] = dot(rounded_ref[:half, :], block_ref[k], NN).astype(bf16)
-        left_ref[k, half:, :] = dot(rounded_ref[half:, half:], block_ref[k, half:, :], NN).astype(bf16)
+        left_ref[k, :half, :] = dot(rounded_ref[...], block_ref[k], NN).astype(bf16)
+        left_ref[k, half:, :] = dot(next_ref[...], block_ref[k, half:, :], NN).astype(bf16)
         stores[k].start()
     for store in stores:
         store.wait()
@@ -322,22 +348,34 @@
         name="gram",
     )(basis)
     pair = pltpu.VMEM((2, rank, rank), bf16)
-    rounded, packed, high, low, moved = pl.pallas_call(
-        leaf_kernel,
+    half = rank // 2
+    grid = lambda rows, columns, dtype: jax.ShapeDtypeStruct((rows, columns), dtype)
+    rounded, packed, high, low, moved, state = pl.pallas_call(
+        first_kernel,
         out_shape=(
-            square(bf16),
-            jax.ShapeDtypeStruct((tall, SIDE), bf16),
-            square(bf16),
-            square(bf16),
+            grid(half, rank, bf16),
+            grid(sum(i * SIDE < half for i, _ in corners(rank)) * SIDE, SIDE, bf16),
+            grid(half, half, bf16),
+            grid(half, half, bf16),
             jax.ShapeDtypeStruct(share_shape, f32),
+            grid(half, rank, f32),
         ),
         scratch_shapes=[work, pair, pair],
-        name="leaf",
+        name="first",
     )(gram, steps)
 
     count = lax.axis_size("sub")
     groups = [list(range(low_end, low_end + group)) for low_end in range(0, count, group)]
     shares = lax.all_to_all(moved.astype(jnp.float16), "sub", 0, 0, axis_index_groups=groups)
+    next_rounded, packed, next_high, next_low = pl.pallas_call(
+        second_kernel,
+        out_shape=(grid(half, half, bf16), grid(tall, SIDE, bf16), grid(half, rank, bf16), grid(half, rank, bf16)),
+        scratch_shapes=[work],
+        name="second",
+    )(state, packed)
+    shares, packed, next_rounded, next_high, next_low = lax.optimization_barrier(
+        (shares, packed, next_rounded, next_high, next_low)
+    )
     columns = lax.axis_size("col")
     mine = [packed]
     for shift in range(2, columns, 2):
@@ -350,7 +388,7 @@
     left = pl.pallas_call(
         left_kernel,
         out_shape=jax.ShapeDtypeStruct(blocks.shape, bf16),
-        in_specs=[near, far],
+        in_specs=[near, near, far],
         out_specs=far,
         scratch_shapes=[
             pltpu.VMEM(blocks.shape, bf16),
@@ -358,7 +396,7 @@
             pltpu.SemaphoreType.DMA((2, slots)),
         ],
         name="left",
-    )(rounded, blocks)
+    )(rounded, next_rounded, blocks)
     mine, left = lax.optimization_barrier((tuple(mine), left))
     mine = jnp.stack(mine)
     other = lax.ppermute(mine, "col", [(i, i ^ 1) for i in range(columns)])
@@ -369,7 +407,7 @@
         out_shape=(square(bf16), jax.ShapeDtypeStruct(basis.shape, bf16)),
         scratch_shapes=[work],
         name="root",
-    )(top, high, low, basis)
+    )(top, high, low, next_high, next_low, basis)
     left, other, root, q_leaf = lax.optimization_barrier((left, other, root, q_leaf))
     coupled = pl.pallas_call(
         right_kernel,

time: 99.5 us -> 101 us (1.015)
  Pallas kernels: 50.5 us -> 52.3 us
  waiting for transfers between devices: 18.3 us -> 19.6 us
  starting transfers between devices: 22.1 us -> 20.9 us
    ppermute x3, waiting for transfers between devices: 0.12 us -> 5.08 us  [shards(): lax.ppermute(packed, 'col', [(i, (i - shift) % columns) for i in range(co...]
    all_to_all x1, waiting for transfers between devices: 6.4 us -> 2.71 us  [shards(): lax.all_to_all(moved.astype(jnp.float16), 'sub', 0, 0, axis_index_groups=...]
    pallas_call x1 -> x2, Pallas kernels: 19.2 us -> 21.1 us  [the longest x1 12.4 us: shards(): pl.pallas_call(first_kernel, out_shape=(grid(half, rank, bf16), grid(sum(...]
    all_to_all x1, starting transfers between devices: 7.84 us -> 6.77 us  [shards(): lax.all_to_all(jnp.broadcast_to(share, shares.shape), 'sub', 0, 0, axis_i...]
  transfers between devices with their start and end apart: 6 -> 6, of which waited for: 3 -> 4; matrix products, arithmetic and copies ran while one was open for 3% -> 3% of each run, Pallas kernels for 23% -> 31%
where the time goes in v4:
time: 101 us; the launch traced here: 100 us
  Pallas kernels  52.3 us (52%)
  starting transfers between devices  20.9 us (21%)
  waiting for transfers between devices  19.6 us (19%)
  other arithmetic  4.94 us (5%)
  between operations  1.59 us (2%)
    pallas_call x1, Pallas kernels, shards(): pl.pallas_call(root_kernel, out_shape=(square(bf16), jax.ShapeDtypeStruct...  17 us
    pallas_call x1, Pallas kernels, shards(): pl.pallas_call(first_kernel, out_shape=(grid(half, rank, bf16), grid(sum(...  12.4 us
    all_to_all x1, waiting for transfers between devices, shards(): lax.all_to_all(jnp.broadcast_to(share, shares.shape), 'sub', 0, 0, axis_i...  11.8 us
    all_to_all x1, starting transfers between devices, shards(): lax.all_to_all(moved.astype(jnp.float16), 'sub', 0, 0, axis_index_groups=...  9.21 us
    pallas_call x1, Pallas kernels, shards(): pl.pallas_call(second_kernel, out_shape=(grid(half, half, bf16), grid(tal...  8.7 us
    all_to_all x1, starting transfers between devices, shards(): lax.all_to_all(jnp.broadcast_to(share, shares.shape), 'sub', 0, 0, axis_i...  6.77 us
    pallas_call x1, Pallas kernels, shards(): pl.pallas_call(right_kernel, out_shape=jax.ShapeDtypeStruct(blocks.shape,...  5.27 us
    pallas_call x1, Pallas kernels, shards(): pl.pallas_call(left_kernel, out_shape=jax.ShapeDtypeStruct(blocks.shape,...  5.2 us
  transfers between devices with their start and end apart: 6, of which 4 were waited for; matrix products, arithmetic and copies ran while one was open for 3% of the time, Pallas kernels for 31%

profile of v4, /device:TPU:12, one launch (start us, length us, event | category | flops | bytes accessed | tf_op | source)
XLA Modules:
  0.0 100.2 jit_solution(10966826132905651244)
XLA Ops:
  0.6 3.8 %gram.1.gram_ref = f32[512,512]{1,0:T(8,128)} custom-call(bf16[2048,512]{1,0:T(8,128)(2,1)} %bitcast.12), custom_call_target="tpu_custom_call" | custom-call | tf_op jit(solution)/shard_map/gram/pallas_call | solution.py:342
  4.4 12.4 %first.1 = (bf16[256,512]{1,0:T(8,128)(2,1)}, bf16[896,128]{1,0:T(8,128)(2,1)}, bf16[256,256]{1,0:T(8,128)(2,1)}, bf16[256,256]{1,0:T(8,128)(2,1)}, f32[16,80,128]{2,1,0:T(8,128)}, /*index=5*/f32[256,512]{1,0:T(8,128)}) custom-call(f32[512,512]{1,0:T(8,128)} %gram.1.gram_ref, bf16[4,512,512]{2,1,0:T(8,128)(2,1)} %bitcast.16), custom_call_target="tpu_custom_call" | custom-call | tf_op jit(solution)/shard_map/first/pallas_call | solution.py:353
  16.8 1.9 %convert_element_type.17 = f16[16,80,128]{2,1,0:T(8,128)(2,1)} convert(f32[16,80,128]{2,1,0:T(8,128)} %get-tuple-element.34) | non-fusion elementwise | flops 163840 | bytes 983040 | tf_op jit(solution)/shard_map/convert_element_type | solution.py:369
  18.7 9.2 %all-to-all-start = ((f16[16,80,128]{2,1,0:T(8,128)(2,1)}), f16[16,80,128]{2,1,0:T(8,128)(2,1)S(1)}, u32[]{:S(2)}, u32[]{:S(2)}) async-start(f16[16,80,128]{2,1,0:T(8,128)(2,1)} %convert_element_type.17), calls=%async_computation | async-start | bytes 655360 | tf_op jit(solution)/shard_map/all_to_all | solution.py:369
  27.9 8.7 %second.1 = (bf16[256,256]{1,0:T(8,128)(2,1)}, bf16[1280,128]{1,0:T(8,128)(2,1)}, bf16[256,512]{1,0:T(8,128)(2,1)}, bf16[256,512]{1,0:T(8,128)(2,1)}) custom-call(f32[256,512]{1,0:T(8,128)} %get-tuple-element.35.state_ref, bf16[896,128]{1,0:T(8,128)(2,1)} %get-tuple-element.36.started_ref), custom_call_target="tpu_custom_call" | custom-call | tf_op jit(solution)/shard_map/second/pallas_call | solution.py:370
  36.6 2.7 %all-to-all-done = f16[16,80,128]{2,1,0:T(8,128)(2,1)S(1)} async-done(((f16[16,80,128]{2,1,0:T(8,128)(2,1)}), f16[16,80,128]{2,1,0:T(8,128)(2,1)S(1)}, u32[]{:S(2)}, u32[]{:S(2)}) %all-to-all-start) | async-done | bytes 327712 | tf_op jit(solution)/shard_map/all_to_all | solution.py:369
  39.3 1.6 %collective-permute-start.2 = (bf16[1280,128]{1,0:T(8,128)(2,1)}, bf16[1280,128]{1,0:T(8,128)(2,1)S(1)}, u32[]{:S(2)}, u32[]{:S(2)}) collective-permute-start(bf16[1280,128]{1,0:T(8,128)(2,1)} %get-tuple-element.47), channel_id=1, source_target_pairs={{0,2},{1,3},{2,4},{3,5},{4,6},{5,7},{6,0},{7,1},{8,10},{9,11},{10,... | collective-permute-start | bytes 983048 | tf_op jit(solution)/shard_map/ppermute | solution.py:382
  40.9 0.9 collective-permute-start.1
  41.8 2.4 %collective-permute-start = (bf16[1280,128]{1,0:T(8,128)(2,1)}, bf16[1280,128]{1,0:T(8,128)(2,1)S(1)}, u32[]{:S(2)}, u32[]{:S(2)}) collective-permute-start(bf16[1280,128]{1,0:T(8,128)(2,1)} %get-tuple-element.47), channel_id=1, source_target_pairs={{0,6},{1,7},{2,0},{3,1},{4,2},{5,3},{6,4},{7,5},{8,14},{9,15},{10,... | collective-permute-start | bytes 983048 | tf_op jit(solution)/shard_map/ppermute | solution.py:382
  44.2 0.6 convert_reduce_fusion
  45.5 0.2 exponential_reduce_fusion
  45.7 0.1 multiply_reduce_fusion
  45.9 0.0 copy-start.2
  45.9 5.2 %left.1.left_hbm = bf16[6,512,512]{2,1,0:T(8,128)(2,1)} custom-call(bf16[256,512]{1,0:T(8,128)(2,1)} %get-tuple-element.45.rounded_ref, bf16[256,256]{1,0:T(8,128)(2,1)} %get-tuple-element.46.next_ref, bf16[6,512,512]{2,1,0:T(8,128)(2,1)} %bitcast.14), custom_call_target="tpu_custom_call" | custom-call | tf_op jit(solution)/shard_map/left/pallas_call | solution.py:388
  51.1 0.0 collective-permute-done.2
  51.1 2.1 %collective-permute-done.1 = bf16[1280,128]{1,0:T(8,128)(2,1)S(1)} collective-permute-done((bf16[1280,128]{1,0:T(8,128)(2,1)}, bf16[1280,128]{1,0:T(8,128)(2,1)S(1)}, u32[]{:S(2)}, u32[]{:S(2)}) %collective-permute-start.1) | collective-permute-done | bytes 327712 | tf_op jit(solution)/shard_map/ppermute | solution.py:382
  53.2 3.0 %collective-permute-done = bf16[1280,128]{1,0:T(8,128)(2,1)S(1)} collective-permute-done((bf16[1280,128]{1,0:T(8,128)(2,1)}, bf16[1280,128]{1,0:T(8,128)(2,1)S(1)}, u32[]{:S(2)}, u32[]{:S(2)}) %collective-permute-start) | collective-permute-done | bytes 327712 | tf_op jit(solution)/shard_map/ppermute | solution.py:382
  56.2 0.0 copy-done.2
  56.2 1.2 %pad_maximum_fusion.mine_hbm = bf16[4,1280,128]{2,1,0:T(8,128)(2,1)} fusion(bf16[1,1280,128]{2,1,0:T(8,128)(2,1)S(1)} %bitcast.18, bf16[1,1280,128]{2,1,0:T(8,128)(2,1)S(1)} %bitcast.19, bf16[1,1280,128]{2,1,0:T(8,128)(2,1)S(1)} %bitcast.20, bf16[1,1280,128]{2,1,0:T(8,128)(2,1)S(1)} %bitcast.17), kind=kLoop, calls=%fused_computation | loop fusion | flops 1966080 | bytes 2621440 | tf_op jit(solution)/shard_map/stack | solution.py:401
  57.4 0.0 collective-permute-start.3
  57.4 0.8 broadcast_in_dim.13
  58.2 6.8 %all-to-all-start.1 = ((f16[16,80,128]{2,1,0:T(8,128)(2,1)}), f16[16,80,128]{2,1,0:T(8,128)(2,1)S(1)}, u32[]{:S(2)}, u32[]{:S(2)}) async-start(f16[16,80,128]{2,1,0:T(8,128)(2,1)} %broadcast_in_dim.13), calls=%async_computation.1 | async-start | bytes 655360 | tf_op jit(solution)/shard_map/all_to_all | solution.py:387
  65.0 11.8 %all-to-all-done.1 = f16[16,80,128]{2,1,0:T(8,128)(2,1)S(1)} async-done(((f16[16,80,128]{2,1,0:T(8,128)(2,1)}), f16[16,80,128]{2,1,0:T(8,128)(2,1)S(1)}, u32[]{:S(2)}, u32[]{:S(2)}) %all-to-all-start.1) | async-done | bytes 327712 | tf_op jit(solution)/shard_map/all_to_all | solution.py:387
  76.8 0.9 convert_multiply_fusion.pieces_ref
  77.7 0.0 copy-start
  77.7 0.0 copy-start.1
  77.7 17.0 %root.1 = (bf16[512,512]{1,0:T(8,128)(2,1)}, bf16[2048,512]{1,0:T(8,128)(2,1)}) custom-call(f32[16,80,128]{2,1,0:T(8,128)} %convert_multiply_fusion.pieces_ref, bf16[256,256]{1,0:T(8,128)(2,1)} %get-tuple-element.54.high_ref, bf16[256,256]{1,0:T(8,128)(2,1)} %get-tuple-element.55.low_ref, bf16[256,512]{1,0:T(8,128)(2,1)} %get-tuple-element.56.next_high_ref, ...), custom_call_target="tpu_custom_call" | custom-call | tf_op jit(solution)/shard_map/root/pallas_call | solution.py:405
  94.7 0.0 collective-permute-done.3.other_hbm
  94.7 0.0 copy-done
  94.7 0.0 copy-done.1
  94.7 5.3 %right.1 = bf16[6,512,512]{2,1,0:T(8,128)(2,1)} custom-call(s32[6]{0:T(128)S(1)} %bitcast.11, bf16[6,512,512]{2,1,0:T(8,128)(2,1)S(1)} %copy-done, bf16[4,1280,128]{2,1,0:T(8,128)(2,1)} %pad_maximum_fusion.mine_hbm, bf16[4,1280,128]{2,1,0:T(8,128)(2,1)} %collective-permute-done.3.other_hbm), custom_call_target="tpu_custom_call" | custom-call | tf_op jit(solution)/shard_map/right/pallas_call | solution.py:412
  (1 shorter events, 0.0 us)
Async XLA Ops:
  18.7 20.6 %all-to-all-start = ((f16[16,80,128]{2,1,0:T(8,128)(2,1)}), f16[16,80,128]{2,1,0:T(8,128)(2,1)S(1)}, u32[]{:S(2)}, u32[]{:S(2)}) async-start(f16[16,80,128]{2,1,0:T(8,128)(2,1)} %convert_element_type.17), calls=%async_computation | async-start | bytes 655360 | tf_op jit(solution)/shard_map/all_to_all | solution.py:369
  39.3 11.8 %collective-permute-start.2 = (bf16[1280,128]{1,0:T(8,128)(2,1)}, bf16[1280,128]{1,0:T(8,128)(2,1)S(1)}, u32[]{:S(2)}, u32[]{:S(2)}) collective-permute-start(bf16[1280,128]{1,0:T(8,128)(2,1)} %get-tuple-element.47), channel_id=1, source_target_pairs={{0,2},{1,3},{2,4},{3,5},{4,6},{5,7},{6,0},{7,1},{8,10},{9,11},{10,... | collective-permute-start | bytes 983048 | tf_op jit(solution)/shard_map/ppermute | solution.py:382
  40.9 12.3 %collective-permute-start.1 = (bf16[1280,128]{1,0:T(8,128)(2,1)}, bf16[1280,128]{1,0:T(8,128)(2,1)S(1)}, u32[]{:S(2)}, u32[]{:S(2)}) collective-permute-start(bf16[1280,128]{1,0:T(8,128)(2,1)} %get-tuple-element.47), channel_id=1, source_target_pairs={{0,4},{1,5},{2,6},{3,7},{4,0},{5,1},{6,2},{7,3},{8,12},{9,13},{10,... | collective-permute-start | bytes 983048 | tf_op jit(solution)/shard_map/ppermute | solution.py:382
  41.8 14.4 %collective-permute-start = (bf16[1280,128]{1,0:T(8,128)(2,1)}, bf16[1280,128]{1,0:T(8,128)(2,1)S(1)}, u32[]{:S(2)}, u32[]{:S(2)}) collective-permute-start(bf16[1280,128]{1,0:T(8,128)(2,1)} %get-tuple-element.47), channel_id=1, source_target_pairs={{0,6},{1,7},{2,0},{3,1},{4,2},{5,3},{6,4},{7,5},{8,14},{9,15},{10,... | collective-permute-start | bytes 983048 | tf_op jit(solution)/shard_map/ppermute | solution.py:382
  45.9 10.3 %copy-start.2 = (bf16[1280,128]{1,0:T(8,128)(2,1)S(1)}, bf16[1280,128]{1,0:T(8,128)(2,1)}, u32[]{:S(2)}) copy-start(bf16[1280,128]{1,0:T(8,128)(2,1)} %get-tuple-element.47) | copy-start | bytes 983044
  57.4 37.3 %collective-permute-start.3 = (bf16[4,1280,128]{2,1,0:T(8,128)(2,1)}, bf16[4,1280,128]{2,1,0:T(8,128)(2,1)}, u32[]{:S(2)}, u32[]{:S(2)}) collective-permute-start(bf16[4,1280,128]{2,1,0:T(8,128)(2,1)} %pad_maximum_fusion.mine_hbm), channel_id=1, source_target_pairs={{0,1},{1,0},{2,3},{3,2},{4,5},{5,4},{6,7},{7,6},{8,9},{9,8},{10,11... | collective-permute-start | bytes 3932168 | tf_op jit(solution)/shard_map/ppermute | solution.py:402
  58.2 18.6 %all-to-all-start.1 = ((f16[16,80,128]{2,1,0:T(8,128)(2,1)}), f16[16,80,128]{2,1,0:T(8,128)(2,1)S(1)}, u32[]{:S(2)}, u32[]{:S(2)}) async-start(f16[16,80,128]{2,1,0:T(8,128)(2,1)} %broadcast_in_dim.13), calls=%async_computation.1 | async-start | bytes 655360 | tf_op jit(solution)/shard_map/all_to_all | solution.py:387
  77.7 17.0 %copy-start = (bf16[6,512,512]{2,1,0:T(8,128)(2,1)S(1)}, bf16[6,512,512]{2,1,0:T(8,128)(2,1)}, u32[]{:S(2)}) copy-start(bf16[6,512,512]{2,1,0:T(8,128)(2,1)} %left.1.left_hbm) | copy-start | bytes 9437188
  77.7 17.0 %copy-start.1 = (s32[1,1,6]{2,1,0:T(1,128)S(1)}, s32[1,1,6]{2,1,0:T(1,128)}, u32[]{:S(2)}) copy-start(s32[1,1,6]{2,1,0:T(1,128)} %param.7) | copy-start | bytes 76
